TPU v7x, 32 devices: a whole 2x2x4 slice. The times are simulated.
32 devices in a mesh: row: 4 (over y, x), col: 4 (over z), depth: 2 (over core).
Axes of the slice: x: 2, y: 2, z: 4, core: 2. Of those that a mesh axis runs over, the one named last changes fastest.
Arguments:
- left_outer: bfloat16 [4, 8, 2048, 128], P('row', 'depth', 'col'), may hold values from -6 to 6
- left_inner: bfloat16 [4, 8, 2048, 128], P('row', 'depth', 'col'), may hold values from -0.125 to 0.125
- right_outer: bfloat16 [4, 8, 2048, 128], P('col', 'depth', 'row'), may hold values from -6 to 6
- right_inner: bfloat16 [4, 8, 2048, 128], P('col', 'depth', 'row'), may hold values from -0.125 to 0.125
- range_test: bfloat16 [4, 2048, 128], P('col', 'row'), may hold values from -0.125 to 0.125
- corange_test: bfloat16 [4, 2048, 256], P('row', 'col'), may hold values from -0.125 to 0.125
- product_mask: int32 [4, 4, 8], P('row', 'col', 'depth'), may hold values 0 or 1
Outputs:
- range_factor: float32 [4, 4, 2048, 128], P('row', 'col', 'depth')
- corange_factor: float32 [4, 4, 2048, 128], P('row', 'col', 'depth')
All inputs are finite; a program needn't handle non-finite values. No bound on the sum of `product_mask` on one device may be relied on, other than what follows from the above.
Results may differ from a plain program's by a relative error of at most 0.0093.
Values may be sent and summed in bfloat16 or wider, within the bound.
A program may use at most 64 MiB of HBM per device.

v0:
```python
import functools

import jax
import jax.numpy as jnp
from jax import lax
from jax.experimental import pallas as pl
from jax.experimental.pallas import tpu as pltpu
from jax.sharding import PartitionSpec as P

F32 = jnp.float32
BF16 = jnp.bfloat16
HIGHEST = lax.Precision.HIGHEST
MESH = pl.DeviceIdType.MESH


def mm(a, b, contract=(1, 0), precision=None):
    dims = (((contract[0],), (contract[1],)), ((), ()))
    return lax.dot_general(a, b, dims, precision=precision, preferred_element_type=F32)


def guarded(cond, action):
    if cond is None:
        action()
    else:
        pl.when(cond)(action)


def inverse_schedule(rank):
    low = 1.0 / (rank / 0.05 + 1.0)
    low *= 0.999
    start = 2.0 / (1.0 + low)
    err = 1.0 - low * start
    scales = []
    while err > 1e-8:
        scales.append(2.0 / (2.0 - err * err))
        err = err * err / (2.0 - err * err)
    return start, scales


def kernel(
    sizes,
    lo, li, ro, ri, rt, ct, mask,
    out_range, out_corange,
    lig, rig, pp, ppr, probe, tp, tpr, test, crt, cps, cpr, zz,
    rps, rpr, rsend, rout, qps, qpr, qsend, qout, ext, xs, xr, cx,
    li_l, li_r, li_in, ri_s, ri_in,
    pp_s, pp_in, pr_s, pr_in, tp_s, tp_in, te_s, te_in,
    cr_s, cr_in, cp_s, cp_in, z_s, z_in,
    rp_s, rp_in, ro_s, ro_in, qp_s, qp_in, qo_s, qo_in, ext_s, ext_in, x_s,
):
    R, C, D, K = sizes
    KR, KC = K // R, K // C
    rank = lo.shape[2]
    r, c, d = lax.axis_index("row"), lax.axis_index("col"), lax.axis_index("depth")
    pending = []

    def copy(src, dst, send, recv, dev, cond=None):
        op = pltpu.make_async_remote_copy(
            src_ref=src, dst_ref=dst, send_sem=send, recv_sem=recv,
            device_id=dev, device_id_type=MESH,
        )
        guarded(cond, op.start)
        pending.append((cond, op))

    def arrive(dst, send, recv, cond=None):
        op = pltpu.make_async_remote_copy(
            src_ref=dst, dst_ref=dst, send_sem=send, recv_sem=recv,
            device_id=(r, c, d), device_id_type=MESH,
        )
        guarded(cond, op.wait_recv)

    def row_peer(o):
        return lax.rem(r + o, R)

    def col_peer(o):
        return lax.rem(c + o, C)

    def depth_peer(o):
        return lax.rem(d + o, D)

    bar = pltpu.get_barrier_semaphore()

    @pl.loop(1, R * D)
    def _(o):
        n = lax.rem(r * D + d + o, R * D)
        pl.semaphore_signal(bar, inc=1, device_id=(n // D, c, lax.rem(n, D)), device_id_type=MESH)

    @pl.loop(1, C * D)
    def _(o):
        n = lax.rem(c * D + d + o, C * D)
        pl.semaphore_signal(bar, inc=1, device_id=(r, n // D, lax.rem(n, D)), device_id_type=MESH)

    pl.semaphore_wait(bar, R * D + C * D - 2)

    moved = K - 1 if C >= 4 else K
    at_end = jnp.logical_or(c == 0, c == C - 1)
    inside = jnp.logical_and(c > 0, c < C - 1)
    helper = jnp.logical_or(c == 1, c == C - 2)
    near_end = 1 + (c // (C - 1)) * (C - 3)
    served = ((c - 1) // max(C - 3, 1)) * (C - 1)

    def send_li(k):
        skip = 1 if k == moved else 0
        copy(li.at[k], lig.at[c, k], li_l.at[0, k], li_in.at[c, k], (r, c - 1, d), c > skip)
        copy(li.at[k], lig.at[c, k], li_r.at[0, k], li_in.at[c, k], (r, c + 1, d), c < C - 1 - skip)

    def send_ri(k):
        if k == moved:
            copy(rig.at[r, k], ext.at[r], ext_s.at[0], ext_in.at[r], (r, near_end, d), at_end)
        for o in range(1, R):
            copy(rig.at[r, k], rig.at[r, k], ri_s.at[o, k], ri_in.at[r, k], (row_peer(o), c, d),
                 inside if k == moved else None)

    def forward_li(o, k):
        skip = 1 if k == moved else 0
        far = c + o
        cond = jnp.logical_and(far < C, c >= skip)
        arrive(lig.at[far, k], li_l.at[o, k], li_in.at[far, k], cond)
        if o < C - 1:
            copy(lig.at[far, k], lig.at[far, k], li_l.at[o, k], li_in.at[far, k],
                 (r, c - 1, d), jnp.logical_and(cond, c > skip))
        near = c - o
        cond = jnp.logical_and(near >= 0, c < C - skip)
        arrive(lig.at[near, k], li_r.at[o, k], li_in.at[near, k], cond)
        if o < C - 1:
            copy(lig.at[near, k], lig.at[near, k], li_r.at[o, k], li_in.at[near, k],
                 (r, c + 1, d), jnp.logical_and(cond, c < C - 1 - skip))

    half = (K + 1) // 2
    for k in range(half):
        send_li(k)
    for k in range(half):
        rig[r, k] = ri[k].T
        send_ri(k)

    ct_rows = ct[...].T
    for k in range(K):
        tp[k] = mm(ct_rows, lo[k]).astype(BF16)
    for o in range(1, C):
        n = col_peer(o)
        copy(tp.at[pl.ds(n * KC, KC)], tpr.at[c], tp_s.at[o], tp_in.at[c], (r, n, d))
    rt_rows = rt[...].T
    for k in range(K):
        pp[k] = mm(rt_rows, ro[k])
    for o in range(1, R):
        n = row_peer(o)
        copy(pp.at[pl.ds(n * KR, KR)], ppr.at[r], pp_s.at[o], pp_in.at[r], (n, c, d))
    for k in range(half, K):
        send_li(k)
    for k in range(half, K):
        rig[r, k] = ri[k].T
        send_ri(k)
    lig[c] = li[...]

    for k in range(K):
        forward_li(1, k)

    if moved < K:
        arrive(ext.at[r], ext_s.at[0], ext_in.at[r], helper)
        for o in range(1, R):
            copy(ext.at[r], ext.at[r], ext_s.at[o], ext_in.at[r], (row_peer(o), c, d), helper)

    total = tp[pl.ds(c * KC, KC)].astype(F32)
    for o in range(1, C):
        n = col_peer(o)
        arrive(tpr.at[n], tp_s.at[o], tp_in.at[n])
        total = total + tpr[n].astype(F32)
    test[c] = total.astype(BF16)
    for o in range(1, C):
        copy(test.at[c], test.at[c], te_s.at[o], te_in.at[c], (r, col_peer(o), d))
    total = pp[pl.ds(r * KR, KR)]
    for o in range(1, R):
        n = row_peer(o)
        arrive(ppr.at[n], pp_s.at[o], pp_in.at[n])
        total = total + ppr[n]
    probe[r] = total.astype(BF16)
    for o in range(1, R):
        copy(probe.at[r], probe.at[r], pr_s.at[o], pr_in.at[r], (row_peer(o), c, d))

    for o in range(2, C - 1):
        for k in range(K):
            forward_li(o, k)

    for k in range(K):
        for o in range(1, R):
            n = row_peer(o)
            arrive(rig.at[n, k], ri_s.at[o, k], ri_in.at[n, k], inside if k == moved else None)

    def cross_of(block, k):
        total = None
        for b in range(C):
            term = mm(block(b), lig[b, k])
            total = term if total is None else total + term
        return total.astype(BF16)

    if moved < K:
        for o in range(1, R):
            n = row_peer(o)
            arrive(ext.at[n], ext_s.at[o], ext_in.at[n], helper)

        @pl.when(helper)
        def _():
            xs[...] = cross_of(lambda b: ext[b], moved)

        copy(xs, xr, x_s.at[0], x_s.at[1], (r, served, d), helper)

        @pl.when(inside)
        def _():
            cx[...] = cross_of(lambda b: rig[b, moved], moved)

    for o in range(1, R):
        n = row_peer(o)
        arrive(probe.at[n], pr_s.at[o], pr_in.at[n])
    for o in range(1, C):
        n = col_peer(o)
        arrive(test.at[n], te_s.at[o], te_in.at[n])

    scale = (K * D) ** -0.5
    core_left = []
    core_part = None
    for k in range(K):
        if C > 2:
            forward_li(C - 1, k)
        if k == moved:
            arrive(xr, x_s.at[0], x_s.at[1], at_end)

            @pl.when(at_end)
            def _():
                cx[...] = xr[...]

            cross = cx[...]
        else:
            cross = cross_of(lambda b: rig[b, k], k)
        weight = mask[0, 0, k].astype(F32) * scale
        right = (mm(probe[k // KR, k % KR], cross) * weight).astype(BF16)
        lanes = pl.ds(k * rank, rank)
        crt[c, :, lanes] = right
        for o in range(1, C):
            copy(crt.at[c, :, lanes], crt.at[c, :, lanes], cr_s.at[o, k], cr_in.at[c, k],
                 (r, col_peer(o), d))
        test_k = test[k // KC, k % KC]
        core_left.append((mm(cross, test_k, (1, 1)) * weight).astype(BF16))
        term = mm(right, test_k, (1, 1))
        core_part = term if core_part is None else core_part + term

    cps[...] = core_part
    for o in range(1, D):
        copy(cps, cpr.at[d], cp_s.at[o], cp_in.at[d], (r, c, depth_peer(o)))
    cpr[d] = core_part
    for o in range(1, D):
        n = depth_peer(o)
        arrive(cpr.at[n], cp_s.at[o], cp_in.at[n])
    core = cpr[0]
    for n in range(1, D):
        core = core + cpr[n]

    gram = mm(core, core, (1, 1), HIGHEST)
    eye = (
        lax.broadcasted_iota(jnp.int32, (rank, rank), 0)
        == lax.broadcasted_iota(jnp.int32, (rank, rank), 1)
    ).astype(F32)
    trace = jnp.sum(gram * eye)
    ridge = 0.05 * trace / rank + 1e-05
    gram = gram + ridge * eye
    start, scales = inverse_schedule(rank)
    first = start / jnp.broadcast_to(trace + ridge, (rank, rank))
    inv = (scales[0] * first) * (2.0 * eye - first * gram)
    for factor in scales[1:]:
        step = 2.0 * eye - mm(gram, inv, precision=HIGHEST)
        inv = factor * mm(inv, step, precision=HIGHEST)
    weights = (mm(inv, core, precision=HIGHEST) * rank**0.5).astype(BF16)

    for k in range(K):
        rows = pl.ds(k * rank, rank)
        zz[r, rows] = mm(core_left[k], weights, (1, 1)).astype(BF16)
        for o in range(1, R):
            copy(zz.at[r, rows], zz.at[r, rows], z_s.at[o, k], z_in.at[r, k], (row_peer(o), c, d))

    part_l = lo.shape[1] // D
    place = c * D + d
    owner, slot = place // C, lax.rem(place, C)
    lo_all = jnp.concatenate([lo[k] for k in range(K)], axis=1)
    for o in range(C):
        j = col_peer(o)
        if o > 0:
            for k in range(K):
                lanes = pl.ds(k * rank, rank)
                arrive(crt.at[j, :, lanes], cr_s.at[o, k], cr_in.at[j, k])
        total = mm(lo_all, crt[j], (1, 1))
        for n in range(D):
            rps[n, j] = total[n * part_l:(n + 1) * part_l]
        for e in range(1, D):
            n = depth_peer(e)
            copy(rps.at[n, j], rpr.at[d, j], rp_s.at[e, o], rp_in.at[d, j], (r, c, n))
    for o in range(C):
        j = col_peer(o)
        total = rps[d, j]
        for e in range(1, D):
            n = depth_peer(e)
            arrive(rpr.at[n, j], rp_s.at[e, o], rp_in.at[n, j])
            total = total + rpr[n, j]
        rsend[j] = total.astype(BF16)
        copy(rsend.at[j], rout.at[slot], ro_s.at[o], ro_in.at[slot], (r, j, owner),
             owner != d if o == 0 else None)

    part_r = ro.shape[1] // D
    place_q = r * D + d
    owner_q, slot_q = place_q // R, lax.rem(place_q, R)
    ro_all = jnp.concatenate([ro[k] for k in range(K)], axis=1)
    for o in range(R):
        i = row_peer(o)
        if o > 0:
            for k in range(K):
                rows = pl.ds(k * rank, rank)
                arrive(zz.at[i, rows], z_s.at[o, k], z_in.at[i, k])
        total = mm(ro_all, zz[i])
        for n in range(D):
            qps[n, i] = total[n * part_r:(n + 1) * part_r]
        for e in range(1, D):
            n = depth_peer(e)
            copy(qps.at[n, i], qpr.at[d, i], qp_s.at[e, o], qp_in.at[d, i], (r, c, n))
    for o in range(R):
        i = row_peer(o)
        total = qps[d, i]
        for e in range(1, D):
            n = depth_peer(e)
            arrive(qpr.at[n, i], qp_s.at[e, o], qp_in.at[n, i])
            total = total + qpr[n, i]
        qsend[i] = total.astype(BF16)
        copy(qsend.at[i], qout.at[slot_q], qo_s.at[o], qo_in.at[slot_q], (i, c, owner_q),
             owner_q != d if o == 0 else None)

    @pl.when(owner == d)
    def _():
        rout[slot] = rsend[c]

    @pl.when(owner_q == d)
    def _():
        qout[slot_q] = qsend[r]

    for q in range(C):
        src = d * C + q
        mine = jnp.logical_and(src // D == c, lax.rem(src, D) == d)
        arrive(rout.at[q], ro_s.at[0], ro_in.at[q], jnp.logical_not(mine))
        out_range[q * part_l:(q + 1) * part_l, :] = rout[q]
    for q in range(R):
        src = d * R + q
        mine = jnp.logical_and(src // D == r, lax.rem(src, D) == d)
        arrive(qout.at[q], qo_s.at[0], qo_in.at[q], jnp.logical_not(mine))
        out_corange[q * part_r:(q + 1) * part_r, :] = qout[q]
    for cond, op in pending:
        guarded(cond, op.wait_send)


def body(sizes, left_outer, left_inner, right_outer, right_inner, range_test, corange_test, product_mask):
    R, C, D = sizes
    K, BL, rank = left_outer.shape[1:]
    BR = right_outer.shape[2]
    sketch = corange_test.shape[2]
    assert R == C and K % R == 0 and BL % D == 0
    KR, KC = K // R, K // C
    dma = pltpu.SemaphoreType.DMA
    vmem = pltpu.VMEM
    scratch = [
        vmem((C, K, BL, rank), BF16),
        vmem((R, K, rank, BR), BF16),
        vmem((K, rank, rank), F32),
        vmem((R, KR, rank, rank), F32),
        vmem((R, KR, rank, rank), BF16),
        vmem((K, sketch, rank), BF16),
        vmem((C, KC, sketch, rank), BF16),
        vmem((C, KC, sketch, rank), BF16),
        vmem((C, rank, K * rank), BF16),
        vmem((rank, sketch), F32),
        vmem((D, rank, sketch), F32),
        vmem((R, K * rank, rank), BF16),
        vmem((D, C, BL // D, rank), F32),
        vmem((D, C, BL // D, rank), F32),
        vmem((C, BL // D, rank), BF16),
        vmem((C, BL // D, rank), BF16),
        vmem((D, R, BR // D, rank), F32),
        vmem((D, R, BR // D, rank), F32),
        vmem((R, BR // D, rank), BF16),
        vmem((R, BR // D, rank), BF16),
        vmem((R, rank, BR), BF16),
        vmem((rank, rank), BF16),
        vmem((rank, rank), BF16),
        vmem((rank, rank), BF16),
        dma((C, K)), dma((C, K)), dma((C, K)), dma((R, K)), dma((R, K)),
        dma((R,)), dma((R,)), dma((R,)), dma((R,)),
        dma((C,)), dma((C,)), dma((C,)), dma((C,)),
        dma((C, K)), dma((C, K)), dma((D,)), dma((D,)), dma((R, K)), dma((R, K)),
        dma((D, C)), dma((D, C)), dma((C,)), dma((C,)),
        dma((D, R)), dma((D, R)), dma((R,)), dma((R,)),
        dma((R,)), dma((R,)), dma((2,)),
    ]
    tile = BL * C
    whole = pl.BlockSpec(memory_space=pltpu.VMEM)
    out = jax.ShapeDtypeStruct((tile // D, rank), BF16)
    range_rows, corange_rows = pl.pallas_call(
        functools.partial(kernel, (R, C, D, K)),
        out_shape=(out, out),
        in_specs=[whole] * 6 + [pl.BlockSpec(memory_space=pltpu.SMEM)],
        out_specs=(whole, whole),
        scratch_shapes=scratch,
        compiler_params=pltpu.CompilerParams(
            collective_id=0, has_side_effects=True, vmem_limit_bytes=60 * 1024 * 1024
        ),
    )(left_outer[0], left_inner[0], right_outer[0], right_inner[0],
      range_test[0], corange_test[0], product_mask)
    return range_rows[None, None].astype(F32), corange_rows[None, None].astype(F32)


def solution(mesh):
    sizes = tuple(mesh.shape[name] for name in ("row", "col", "depth"))
    return jax.shard_map(
        functools.partial(body, sizes),
        mesh=mesh,
        in_specs=(
            P("row", "depth", "col", None),
            P("row", "depth", "col", None),
            P("col", "depth", "row", None),
            P("col", "depth", "row", None),
            P("col", "row", None),
            P("row", "col", None),
            P("row", "col", "depth"),
        ),
        out_specs=(P("row", "col", "depth", None), P("row", "col", "depth", None)),
        check_vma=False,
    )
```

profile of v0, /device:TPU:0, one launch (start us, length us, event | category | flops | bytes accessed | tf_op | source)
XLA Modules:
  0.0 70.5 jit_solution(8221352690905204683)
XLA Ops:
  0.6 67.8 %shard_map.86 = (bf16[1024,128]{1,0:T(8,128)(2,1)}, bf16[1024,128]{1,0:T(8,128)(2,1)}) custom-call(bf16[4,512,128]{2,1,0:T(8,128)(2,1)} %bitcast.12, bf16[4,512,128]{2,1,0:T(8,128)(2,1)} %bitcast.13, bf16[4,512,128]{2,1,0:T(8,128)(2,1)} %bitcast.14, bf16[4,512,128]{2,1,0:T(8,128)(2,1)} %bitcast.15, bf16[512,128]{1,0:T(8,128)(2,1)} %bitcast.17, ...), custom_call_target="tpu_custom_call" | custom-call | tf_op jit(solution)/shard_map/pallas_call | solution.py:400
  68.4 2.1 %bitcast_convert_fusion = (f32[1,1,1024,128]{3,2,1,0:T(8,128)}, f32[1,1,1024,128]{3,2,1,0:T(8,128)}) fusion(bf16[1024,128]{1,0:T(8,128)(2,1)} %get-tuple-element.5, bf16[1024,128]{1,0:T(8,128)(2,1)} %get-tuple-element.4), kind=kLoop, calls=%fused_computation | loop fusion | flops 262144 | bytes 1572864 | tf_op jit(solution)/shard_map/convert_element_type | solution.py:411
where the time goes:
time: 70.6 us; the launch traced here: 70.5 us
  Pallas kernels  67.8 us (96%)
  other arithmetic  2.07 us (3%)
    pallas_call x1, Pallas kernels, body(): pl.pallas_call(functools.partial(kernel, (R, C, D, K)), out_shape=(out, o...  67.8 us
    convert_element_type x1, other arithmetic, body(): corange_rows[None, None].astype(F32)  2.07 us

commit v1 on v0

v1 whole, which is shorter than its diff:
```python
import functools

import jax
import jax.numpy as jnp
from jax import lax
from jax.experimental import pallas as pl
from jax.experimental.pallas import tpu as pltpu
from jax.sharding import PartitionSpec as P

F32 = jnp.float32
BF16 = jnp.bfloat16
HIGHEST = lax.Precision.HIGHEST
MESH = pl.DeviceIdType.MESH
RULER = 32768


def mm(a, b, contract=(1, 0), precision=None):
    dims = (((contract[0],), (contract[1],)), ((), ()))
    return lax.dot_general(a, b, dims, precision=precision, preferred_element_type=F32)


def inverse_schedule(rank):
    low = 1.0 / (rank / 0.05 + 1.0)
    low *= 0.999
    start = 2.0 / (1.0 + low)
    err = 1.0 - low * start
    scales = []
    while err > 1e-3:
        scales.append(2.0 / (2.0 - err * err))
        err = err * err / (2.0 - err * err)
    return start, scales


def kernel(
    sizes,
    lo_h, li_h, ro_h, ri_h, rt_h, ct_h, mask_h,
    out_range, out_corange,
    mask, ruler, lo, ro, ri, rt, ct, lig, rig, rx, tp, tpe, tps, tpo, test, tmid, pps, ppr, probe,
    cx, xs, xr, cps, cpr, crt, clt, zz, rps, rpr, rsend, rout, qps, qpr, qsend, qout,
    load_s, send_s, li_in, ri_in, ext_in, tp_in, te_in, pp_in, pr_in, xr_in, cp_in, cr_in, z_in,
    rp_in, ro_in, qp_in, qo_in,
):
    R, C, D, K = sizes
    KM = K // 2
    KN = K - KM
    KR = K // R
    rank = lo_h.shape[2]
    r, c, d = lax.axis_index("row"), lax.axis_index("col"), lax.axis_index("depth")
    is_end = jnp.logical_or(c == 0, c == C - 1)
    is_mid = jnp.logical_not(is_end)
    across = (r + 1 - 2 * lax.rem(r, 2), lax.rem(r + 2, R), R - 1 - r)
    sent = {}

    def send(branch, src, dst, recv, dev, size, sem=0):
        op = pltpu.make_async_remote_copy(
            src_ref=src, dst_ref=dst, send_sem=send_s.at[sem], recv_sem=recv,
            device_id=dev, device_id_type=MESH,
        )
        op.start()
        sent[branch] = sent.get(branch, 0) + size

    def arrive(ref, recv):
        pltpu.make_async_remote_copy(
            src_ref=ref, dst_ref=ref, send_sem=send_s.at[0], recv_sem=recv,
            device_id=(r, c, d), device_id_type=MESH,
        ).wait_recv()

    def drain(sem, ref):
        pltpu.make_async_remote_copy(
            src_ref=ref, dst_ref=ref, send_sem=send_s.at[sem], recv_sem=load_s.at[0],
            device_id=(r, c, d), device_id_type=MESH,
        ).wait_send()

    def bytes_of(size):
        return ruler.at[pl.ds(0, size // (2 * rank))]

    def load(src, dst, index):
        op = pltpu.make_async_copy(src, dst, load_s.at[index])
        op.start()
        return op

    load_ri = load(ri_h, ri, 0)
    load_ct = load(ct_h, ct, 1)
    for k in range(K):
        load(lo_h.at[k], lo.at[:, pl.ds(k * rank, rank)], 2)
    load_rt = load(rt_h, rt, 3)
    for k in range(K):
        load(ro_h.at[k], ro.at[:, pl.ds(k * rank, rank)], 4)
    load_li = load(li_h, lig.at[c], 5)
    load_mask = load(mask_h, mask, 6)

    bar = pltpu.get_barrier_semaphore()

    @pl.loop(1, R * D)
    def _(o):
        n = lax.rem(r * D + d + o, R * D)
        pl.semaphore_signal(bar, inc=1, device_id=(n // D, c, lax.rem(n, D)), device_id_type=MESH)

    @pl.loop(1, C * D)
    def _(o):
        n = lax.rem(c * D + d + o, C * D)
        pl.semaphore_signal(bar, inc=1, device_id=(r, n // D, lax.rem(n, D)), device_id_type=MESH)

    pl.semaphore_wait(bar, R * D + C * D - 2)

    BLK = lig.shape[2] * rank * 2
    SQ = rank * rank * 2
    sketch = ct_h.shape[1]
    near = 1 + (c // (C - 1)) * (C - 3)
    edge = ((c - 1) // max(C - 3, 1)) * (C - 1)
    other = C - 1 - c
    half = KM * rank

    def send_li(branch, k, owner, dev, src=None):
        send(branch, lig.at[owner, k] if src is None else src, lig.at[owner, k],
             li_in.at[owner, k], dev, BLK)

    def send_ri(branch, k, owner, to, slot):
        send(branch, rig.at[owner, k], rig.at[owner, k], ri_in.at[slot, k], (to, c, d), BLK)

    def relay_ri(branch, k):
        via, to = (0, 1) if k % 2 == 0 else (1, 0)
        arrive(rig.at[across[via], k], ri_in.at[via, k])
        send_ri(branch, k, across[via], across[to], 2)

    def wait_ri(k, skip):
        for slot in range(3):
            if slot != skip:
                arrive(rig.at[across[slot], k], ri_in.at[slot, k])

    def via_of(k):
        return 0 if k % 2 == 0 else 1

    def tall(ref_row, kk, part):
        return rx.at[ref_row, kk, pl.ds(part * rank, rank)]

    def send_x(branch, kk, part, owner, to, slot):
        send(branch, tall(owner, kk, part), tall(owner, kk, part), ext_in.at[part, slot, kk],
             (to, c, d), BLK)

    def relay_x(branch, kk, part):
        via, to = (0, 1) if kk % 2 == 0 else (1, 0)
        arrive(tall(across[via], kk, part), ext_in.at[part, via, kk])
        send_x(branch, kk, part, across[via], across[to], 2)

    def tests():
        load_ct.wait()
        pltpu.make_async_copy(lo, lo, load_s.at[2]).wait()
        tp[...] = mm(ct[...].T, lo[...]).astype(BF16)

    def probes(branch):
        load_rt.wait()
        pltpu.make_async_copy(ro, ro, load_s.at[4]).wait()
        part = mm(rt[...].T, ro[...])
        for n in range(R):
            pps[n] = part[:, n * KR * rank:(n + 1) * KR * rank]
        for slot in range(3):
            send(branch, pps.at[across[slot]], ppr.at[slot], pp_in.at[0],
                 (across[slot], c, d), KR * SQ * 2)

    def probe_sum(branch):
        arrive(ppr, pp_in.at[0])
        total = pps[r]
        for slot in range(3):
            total = total + ppr[slot]
        probe[r] = total.astype(BF16)
        for slot in range(3):
            send(branch, probe.at[r], probe.at[r], pr_in.at[0], (across[slot], c, d), KR * SQ)

    def probe_wait():
        arrive(probe.at[pl.ds(0, 3)], pr_in.at[0])

    scale = (K * D) ** -0.5

    def cross_plain(k):
        total = None
        for b in range(C):
            term = mm(rig[b, k], lig[b, k])
            total = term if total is None else total + term
        return total.astype(BF16)

    def right_of(k, cross):
        weight = mask[0, 0, k].astype(F32) * scale
        lanes = pl.ds(k % KR * rank, rank)
        right = (mm(probe[k // KR, :, lanes], cross) * weight).astype(BF16)
        crt[c, :, pl.ds(k * rank, rank)] = right

    def part_of(n, part):
        return crt.at[n, :, pl.ds(0, KN * rank) if part == 0 else pl.ds(KN * rank, half)]

    def send_crt(branch, owner, part, to):
        send(branch, part_of(owner, part), part_of(owner, part), cr_in.at[owner, part],
             (r, to, d), (KN if part == 0 else KM) * SQ)

    @pl.when(is_mid)
    def _():
        B = "mid"
        for k in range(K):
            send_li(B, k, c, (r, other, d), li_h.at[k])
            if k < KN:
                send_li(B, k, c, (r, edge, d), li_h.at[k])
        load_ri.wait()
        for k in range(KN):
            rig[r, k] = ri[k].T
            for slot in range(2):
                send_ri(B, k, r, across[slot], slot)
        for kk in range(KM):
            rx[r, kk, 0:rank] = ri[KN + kk].T
            for slot in range(2):
                send_x(B, kk, 0, r, across[slot], slot)
        tests()
        probes(B)
        far = C - 1 - edge
        lower = c == 1
        h = jnp.where(lower, 0, 1)
        arrive(lig.at[edge, 0], li_in.at[edge, 0])
        send_li(B, 0, edge, (r, other, d))
        for k in range(KN):
            arrive(lig.at[other, k], li_in.at[other, k])
            send_li(B, k, other, (r, edge, d))
            relay_ri(B, k)
        arrive(tpe, tp_in.at[0])
        both = tpe[...].astype(F32) + tp[...].astype(F32)
        tmid[...] = jnp.where(lower, both[:, 0:half], both[:, half:2 * half])
        tps[...] = jnp.where(lower, both[:, half:2 * half], both[:, 0:half]).astype(BF16)
        send(B, tps, tpo, tp_in.at[1], (r, other, d), sketch * half * 2)
        for k in range(1, KN):
            arrive(lig.at[edge, k], li_in.at[edge, k])
            send_li(B, k, edge, (r, other, d))
        relay_x(B, 0, 0)
        relay_x(B, 1, 0)
        arrive(tall(r, 0, 1), ext_in.at[1, 3, 0])
        for slot in range(2):
            send_x(B, 0, 1, r, across[slot], slot)
        arrive(lig.at[far, 0], li_in.at[far, 0])
        send_li(B, 0, far, (r, edge, d))
        arrive(tpo, tp_in.at[1])
        test[h] = (tmid[...] + tpo[...].astype(F32)).astype(BF16)
        for to in (edge, other):
            send(B, test.at[h], test.at[h], te_in.at[h], (r, to, d), sketch * half * 2)
        arrive(tall(r, 1, 1), ext_in.at[1, 3, 1])
        for slot in range(2):
            send_x(B, 1, 1, r, across[slot], slot)
        probe_sum(B)
        arrive(lig.at[edge, KN], li_in.at[edge, KN])
        send_li(B, KN, edge, (r, other, d))
        for k in range(1, KN):
            arrive(lig.at[far, k], li_in.at[far, k])
            send_li(B, k, far, (r, edge, d))
        for k in range(KN + 1, K):
            arrive(lig.at[edge, k], li_in.at[edge, k])
            send_li(B, k, edge, (r, other, d))
        arrive(test.at[1 - h], te_in.at[1 - h])
        send(B, test.at[1 - h], test.at[1 - h], te_in.at[1 - h], (r, edge, d), sketch * half * 2)
        for kk in range(KM):
            relay_x(B, kk, 1)
        for k in range(KN):
            wait_ri(k, via_of(k))
        probe_wait()
        load_li.wait()
        load_mask.wait()
        for k in range(KN):
            cx[k] = cross_plain(k)
            right_of(k, cx[k])
        for to in (other, edge):
            send_crt(B, c, 0, to)
        for kk in range(KM):
            k = KN + kk
            for part in range(2):
                for slot in range(3):
                    if slot != via_of(kk):
                        arrive(tall(across[slot], kk, part), ext_in.at[part, slot, kk])
            for b in (other, far):
                arrive(lig.at[b, k], li_in.at[b, k])
            total = None
            for b in range(C):
                term = mm(rx[b, kk], lig[b, k])
                total = term if total is None else total + term
            xs[kk] = total[rank:].astype(BF16)
            send(B, xs.at[kk], xr.at[kk], xr_in.at[kk], (r, edge, d), SQ)
            cx[k] = total[:rank].astype(BF16)
        for k in range(KN, K):
            right_of(k, cx[k])
        for to in (edge, other, far):
            send_crt(B, c, 1, to)

    @pl.when(is_end)
    def _():
        B = "end"
        send_li(B, 0, c, (r, near, d), li_h.at[0])
        load_ri.wait()
        for k in range(KN):
            rig[r, k] = ri[k].T
            for slot in range(2):
                send_ri(B, k, r, across[slot], slot)
        tests()
        send(B, tp, tpe, tp_in.at[0], (r, near, d), sketch * K * rank * 2)
        for k in range(1, KN):
            send_li(B, k, c, (r, near, d), li_h.at[k])
        for kk in range(KM):
            rx[r, kk, 0:rank] = ri[KN + kk].T
            send(B, tall(r, kk, 0), tall(r, kk, 1), ext_in.at[1, 3, kk], (r, near, d), BLK)
        for k in range(KN, K):
            send_li(B, k, c, (r, near, d), li_h.at[k])
        probes(B)
        for k in range(KN):
            relay_ri(B, k)
        probe_sum(B)
        for n in (near, C - 1 - near, other):
            for k in range(KN):
                arrive(lig.at[n, k], li_in.at[n, k])
        for k in range(KN):
            wait_ri(k, via_of(k))
        probe_wait()
        load_li.wait()
        load_mask.wait()
        for k in range(KN):
            cx[k] = cross_plain(k)
            right_of(k, cx[k])
        send_crt(B, c, 0, near)
        for h in range(2):
            arrive(test.at[h], te_in.at[h])
        for kk in range(KM):
            arrive(xr.at[kk], xr_in.at[kk])
            cx[KN + kk] = xr[kk]
            right_of(KN + kk, xr[kk])
        for to in (near, C - 1 - near, other):
            send_crt(B, c, 1, to)

    core_part = None
    for k in range(K):
        weight = mask[0, 0, k].astype(F32) * scale
        hk, kk = (0, k) if k < KN else (1, k - KN)
        test_k = test[hk, :, kk * rank:(kk + 1) * rank]
        clt[k] = (mm(cx[k], test_k, (1, 1)) * weight).astype(BF16)
        term = mm(crt[c, :, k * rank:(k + 1) * rank], test_k, (1, 1))
        core_part = term if core_part is None else core_part + term
    cps[...] = core_part
    for o in range(1, D):
        send("cp", cps, cpr.at[d], cp_in.at[0], (r, c, lax.rem(d + o, D)), 0, 3)
    cpr[d] = core_part

    @pl.when(is_mid)
    def _():
        B = "mid"
        arrive(part_of(edge, 0), cr_in.at[edge, 0])
        send_crt(B, edge, 0, other)
        arrive(part_of(other, 0), cr_in.at[other, 0])
        send_crt(B, other, 0, edge)

    arrive(cpr.at[pl.ds(0, D - 1)], cp_in.at[0])
    core = cpr[0]
    for n in range(1, D):
        core = core + cpr[n]

    gram = mm(core, core, (1, 1), HIGHEST)
    eye = (
        lax.broadcasted_iota(jnp.int32, (rank, rank), 0)
        == lax.broadcasted_iota(jnp.int32, (rank, rank), 1)
    ).astype(F32)
    trace = jnp.sum(core * core)
    ridge = 0.05 * trace / rank + 1e-05
    norm = 1.0 / jnp.broadcast_to(trace + ridge, (rank, rank))
    gram = (gram + ridge * eye) * norm
    start, scales = inverse_schedule(rank)
    rest = eye - start * gram
    inv = (scales[0] * start) * (eye + rest)
    rest = (1.0 - scales[0]) * eye + scales[0] * mm(rest, rest, precision=HIGHEST)
    for factor in scales[1:]:
        both = mm(jnp.concatenate([inv, rest], axis=0), rest, precision=HIGHEST)
        inv = factor * (inv + both[:rank])
        rest = (1.0 - factor) * eye + factor * both[rank:]
    for _ in range(1):
        inv = inv + mm(inv, eye - mm(gram, inv, precision=HIGHEST), precision=HIGHEST)
    weights = (mm(inv, core, precision=HIGHEST) * (norm[:, 0:1] * rank**0.5)).astype(BF16)

    rows = KN * rank

    def zpart(n, part):
        return zz.at[n, pl.ds(0, rows) if part == 0 else pl.ds(rows, half)]

    for part in range(2):
        for k in range(KN) if part == 0 else range(KN, K):
            zz[r, pl.ds(k * rank, rank)] = mm(clt[k], weights, (1, 1)).astype(BF16)
        for slot in range(2):
            send("all", zpart(r, part), zpart(r, part), z_in.at[slot, part], (across[slot], c, d),
                 (KN if part == 0 else KM) * SQ)

    @pl.when(is_mid)
    def _():
        B = "mid"
        far = C - 1 - edge
        arrive(part_of(far, 0), cr_in.at[far, 0])
        send_crt(B, far, 0, edge)

    def relay_z(part):
        via, to = (0, 1) if part == 0 else (1, 0)
        arrive(zpart(across[via], part), z_in.at[via, part])
        send("all", zpart(across[via], part), zpart(across[via], part), z_in.at[2, part],
             (across[to], c, d), (KN if part == 0 else KM) * SQ)

    part_l = lo_h.shape[1] // D
    place = c * D + d
    owner, slot_l = place // C, lax.rem(place, C)

    def range_mm(j, index):
        total = mm(lo[...], crt[j], (1, 1))
        for n in range(D):
            rps[n, index] = total[n * part_l:(n + 1) * part_l]
        for e in range(1, D):
            n = lax.rem(d + e, D)
            send("rp", rps.at[n, index], rpr.at[index, d], rp_in.at[index], (r, c, n), 0, 4)

    def range_out(j, index, first):
        total = rps[d, index]
        arrive(rpr.at[index, pl.ds(0, D - 1)], rp_in.at[index])
        for e in range(1, D):
            total = total + rpr[index, lax.rem(d + e, D)]
        rsend[index] = total.astype(BF16)
        if first:
            @pl.when(owner != d)
            def _():
                send("ro", rsend.at[index], rout.at[slot_l], ro_in.at[slot_l], (r, j, owner), part_l * rank * 2, 1)
        else:
            send("all", rsend.at[index], rout.at[slot_l], ro_in.at[slot_l], (r, j, owner), part_l * rank * 2)

    range_mm(c, 0)
    relay_z(0)
    relay_z(1)

    for o in range(1, C):
        n = lax.rem(c + o, C)
        arrive(part_of(n, 1), cr_in.at[n, 1])

    @pl.when(is_end)
    def _():
        for o in range(1, C):
            n = lax.rem(c + o, C)
            arrive(part_of(n, 0), cr_in.at[n, 0])

    for o in range(1, C):
        range_mm(lax.rem(c + o, C), o)
    for o in range(C):
        range_out(lax.rem(c + o, C), o, o == 0)

    part_r = ro_h.shape[1] // D
    place_q = r * D + d
    owner_q, slot_q = place_q // R, lax.rem(place_q, R)

    def corange_mm(i, index):
        total = mm(ro[...], zz[i])
        for n in range(D):
            qps[n, index] = total[n * part_r:(n + 1) * part_r]
        for e in range(1, D):
            n = lax.rem(d + e, D)
            send("qp", qps.at[n, index], qpr.at[index, d], qp_in.at[index], (r, c, n), 0, 5)

    def corange_out(i, index, first):
        total = qps[d, index]
        arrive(qpr.at[index, pl.ds(0, D - 1)], qp_in.at[index])
        for e in range(1, D):
            total = total + qpr[index, lax.rem(d + e, D)]
        qsend[index] = total.astype(BF16)
        if first:
            @pl.when(owner_q != d)
            def _():
                send("qo", qsend.at[index], qout.at[slot_q], qo_in.at[slot_q], (i, c, owner_q), part_r * rank * 2, 2)
        else:
            send("all", qsend.at[index], qout.at[slot_q], qo_in.at[slot_q], (i, c, owner_q), part_r * rank * 2)

    corange_mm(r, 0)
    arrive(zpart(across[0], 1), z_in.at[0, 1])
    corange_mm(across[0], 1)
    arrive(zpart(across[1], 0), z_in.at[1, 0])
    corange_mm(across[1], 2)
    for part in range(2):
        arrive(zpart(across[2], part), z_in.at[2, part])
    corange_mm(across[2], 3)
    corange_out(r, 0, True)
    for slot in range(3):
        corange_out(across[slot], slot + 1, False)

    @pl.when(owner == d)
    def _():
        rout[slot_l] = rsend[0]

    @pl.when(owner_q == d)
    def _():
        qout[slot_q] = qsend[0]

    for q in range(C):
        src = d * C + q
        mine = jnp.logical_and(src // D == c, lax.rem(src, D) == d)

        @pl.when(jnp.logical_not(mine))
        def _(q=q):
            arrive(rout.at[q], ro_in.at[q])

        out_range[q * part_l:(q + 1) * part_l, :] = rout[q]
    for q in range(R):
        src = d * R + q
        mine = jnp.logical_and(src // D == r, lax.rem(src, D) == d)

        @pl.when(jnp.logical_not(mine))
        def _(q=q):
            arrive(qout.at[q], qo_in.at[q])

        out_corange[q * part_r:(q + 1) * part_r, :] = qout[q]

    drain(3, cpr.at[pl.ds(0, D - 1)])
    drain(4, rpr.at[:, pl.ds(0, D - 1)])
    drain(5, qpr.at[:, pl.ds(0, D - 1)])
    for branch, cond in (("mid", is_mid), ("end", is_end)):
        @pl.when(cond)
        def _(branch=branch):
            drain(0, bytes_of(sent["all"] + sent[branch]))
    for branch, cond, sem in (("ro", owner != d, 1), ("qo", owner_q != d, 2)):
        @pl.when(cond)
        def _(branch=branch, sem=sem):
            drain(sem, bytes_of(sent[branch]))


def body(sizes, left_outer, left_inner, right_outer, right_inner, range_test, corange_test, product_mask):
    R, C, D = sizes
    K, BL, rank = left_outer.shape[1:]
    BR = right_outer.shape[2]
    sketch = corange_test.shape[2]
    assert R == 4 and C == 4 and K % R == 0 and BL == BR and BL % D == 0 and D > 1
    KM = K // 2
    KN = K - KM
    KR = K // R
    dma = pltpu.SemaphoreType.DMA
    vmem = pltpu.VMEM
    scratch = [
        pltpu.SMEM((1, 1, K), jnp.int32),
        vmem((RULER, rank), BF16),
        vmem((BL, K * rank), BF16),
        vmem((BR, K * rank), BF16),
        vmem((K, BR, rank), BF16),
        vmem((BR, rank), BF16),
        vmem((BL, sketch), BF16),
        vmem((C, K, BL, rank), BF16),
        vmem((R, KN, rank, BR), BF16),
        vmem((R, KM, 2 * rank, BR), BF16),
        vmem((sketch, K * rank), BF16),
        vmem((sketch, K * rank), BF16),
        vmem((sketch, KM * rank), BF16),
        vmem((sketch, KM * rank), BF16),
        vmem((2, sketch, KM * rank), BF16),
        vmem((sketch, KM * rank), F32),
        vmem((R, rank, KR * rank), F32),
        vmem((R - 1, rank, KR * rank), F32),
        vmem((R, rank, KR * rank), BF16),
        vmem((K, rank, rank), BF16),
        vmem((KM, rank, rank), BF16),
        vmem((KM, rank, rank), BF16),
        vmem((rank, sketch), F32),
        vmem((D, rank, sketch), F32),
        vmem((C, rank, K * rank), BF16),
        vmem((K, rank, sketch), BF16),
        vmem((R, K * rank, rank), BF16),
        vmem((D, C, BL // D, rank), F32),
        vmem((C, D, BL // D, rank), F32),
        vmem((C, BL // D, rank), BF16),
        vmem((C, BL // D, rank), BF16),
        vmem((D, R, BR // D, rank), F32),
        vmem((R, D, BR // D, rank), F32),
        vmem((R, BR // D, rank), BF16),
        vmem((R, BR // D, rank), BF16),
        dma((7,)), dma((6,)),
        dma((C, K)), dma((3, KN)), dma((2, 4, KM)), dma((2,)), dma((2,)), dma((1,)), dma((1,)), dma((KM,)),
        dma((1,)), dma((C, 2)), dma((3, 2)), dma((C,)), dma((C,)), dma((R,)), dma((R,)),
    ]
    whole = pl.BlockSpec(memory_space=pltpu.VMEM)
    out = jax.ShapeDtypeStruct((BL * C // D, rank), BF16)
    range_rows, corange_rows = pl.pallas_call(
        functools.partial(kernel, (R, C, D, K)),
        out_shape=(out, out),
        in_specs=[pl.BlockSpec(memory_space=pltpu.HBM)] * 7,
        out_specs=(whole, whole),
        scratch_shapes=scratch,
        compiler_params=pltpu.CompilerParams(
            collective_id=0, has_side_effects=True, vmem_limit_bytes=36 * 1024 * 1024
        ),
    )(*[
        pltpu.with_memory_space_constraint(x, pltpu.HBM)
        for x in (left_outer[0], left_inner[0], right_outer[0], right_inner[0],
                  range_test[0], corange_test[0], product_mask)
    ])
    return range_rows[None, None].astype(F32), corange_rows[None, None].astype(F32)


def solution(mesh):
    sizes = tuple(mesh.shape[name] for name in ("row", "col", "depth"))
    return jax.shard_map(
        functools.partial(body, sizes),
        mesh=mesh,
        in_specs=(
            P("row", "depth", "col", None),
            P("row", "depth", "col", None),
            P("col", "depth", "row", None),
            P("col", "depth", "row", None),
            P("col", "row", None),
            P("row", "col", None),
            P("row", "col", "depth"),
        ),
        out_specs=(P("row", "col", "depth", None), P("row", "col", "depth", None)),
        check_vma=False,
    )
```

time: 70.6 us -> 63.5 us (0.90)
  the two profiles are of different devices: /device:TPU:0 before, /device:TPU:1 now
where the time goes in v1:
time: 63.5 us; the launch traced here: 63.3 us
  Pallas kernels  61.7 us (97%)
  other arithmetic  1.04 us (2%)
  between operations  0.64 us (1%)
    pallas_call x1, Pallas kernels, body(): pl.pallas_call(functools.partial(kernel, (R, C, D, K)), out_shape=(out, o...  61.7 us

profile of v1, /device:TPU:1, one launch (start us, length us, event | category | flops | bytes accessed | tf_op | source)
XLA Modules:
  0.0 63.3 jit_solution(470232539541286295)
XLA Ops:
  0.6 61.7 %shard_map.86 = (bf16[1024,128]{1,0:T(8,128)(2,1)S(1)}, bf16[1024,128]{1,0:T(8,128)(2,1)S(1)}) custom-call(bf16[4,512,128]{2,1,0:T(8,128)(2,1)} %bitcast.12, bf16[4,512,128]{2,1,0:T(8,128)(2,1)} %bitcast.13, bf16[4,512,128]{2,1,0:T(8,128)(2,1)} %bitcast.14, bf16[4,512,128]{2,1,0:T(8,128)(2,1)} %bitcast.15, bf16[512,128]{1,0:T(8,128)(2,1)} %bitcast.17, ...), custom_call_target="tpu_custom_call" | custom-call | tf_op jit(solution)/shard_map/pallas_call | solution.py:576
  62.3 1.0 %bitcast_convert_fusion = (f32[1,1,1024,128]{3,2,1,0:T(8,128)}, f32[1,1,1024,128]{3,2,1,0:T(8,128)}) fusion(bf16[1024,128]{1,0:T(8,128)(2,1)S(1)} %get-tuple-element.5, bf16[1024,128]{1,0:T(8,128)(2,1)S(1)} %get-tuple-element.4), kind=kLoop, calls=%fused_computation | loop fusion | flops 262144 | bytes 1572864 | tf_op jit(solution)/shard_map/convert_element_type | solution.py:590

commit v2 on v1

--- a/solution.py
+++ b/solution.py
@@ -17,6 +17,12 @@
 def mm(a, b, contract=(1, 0), precision=None):
     dims = (((contract[0],), (contract[1],)), ((), ()))
     return lax.dot_general(a, b, dims, precision=precision, preferred_element_type=F32)
+
+
+def mm_split(a, b):
+    a_up, b_up = a.astype(BF16), b.astype(BF16)
+    a_low, b_low = (a - a_up.astype(F32)).astype(BF16), (b - b_up.astype(F32)).astype(BF16)
+    return mm(jnp.concatenate([a_up, a_up, a_low], axis=1), jnp.concatenate([b_up, b_low, b_up], axis=0))
 
 
 def inverse_schedule(rank):
@@ -35,7 +41,7 @@
     sizes,
     lo_h, li_h, ro_h, ri_h, rt_h, ct_h, mask_h,
     out_range, out_corange,
-    mask, ruler, lo, ro, ri, rt, ct, lig, rig, rx, tp, tpe, tps, tpo, test, tmid, pps, ppr, probe,
+    mask, ruler, lo, ro, ri, rt, ct, lig, rig, rx, qx, ex, tp, tpe, tps, tpo, test, tmid, pps, ppr, probe,
     cx, xs, xr, cps, cpr, crt, clt, zz, rps, rpr, rsend, rout, qps, qpr, qsend, qout,
     load_s, send_s, li_in, ri_in, ext_in, tp_in, te_in, pp_in, pr_in, xr_in, cp_in, cr_in, z_in,
     rp_in, ro_in, qp_in, qo_in,
@@ -43,6 +49,7 @@
     R, C, D, K = sizes
     KM = K // 2
     KN = K - KM
+    KQ = KN // 2
     KR = K // R
     rank = lo_h.shape[2]
     r, c, d = lax.axis_index("row"), lax.axis_index("col"), lax.axis_index("depth")
@@ -116,17 +123,17 @@
              li_in.at[owner, k], dev, BLK)
 
     def send_ri(branch, k, owner, to, slot):
-        send(branch, rig.at[owner, k], rig.at[owner, k], ri_in.at[slot, k], (to, c, d), BLK)
+        send(branch, rig.at[owner, k - KQ], rig.at[owner, k - KQ], ri_in.at[slot, k - KQ], (to, c, d), BLK)
 
     def relay_ri(branch, k):
         via, to = (0, 1) if k % 2 == 0 else (1, 0)
-        arrive(rig.at[across[via], k], ri_in.at[via, k])
+        arrive(rig.at[across[via], k - KQ], ri_in.at[via, k - KQ])
         send_ri(branch, k, across[via], across[to], 2)
 
     def wait_ri(k, skip):
         for slot in range(3):
             if slot != skip:
-                arrive(rig.at[across[slot], k], ri_in.at[slot, k])
+                arrive(rig.at[across[slot], k - KQ], ri_in.at[slot, k - KQ])
 
     def via_of(k):
         return 0 if k % 2 == 0 else 1
@@ -139,9 +146,23 @@
              (to, c, d), BLK)
 
     def relay_x(branch, kk, part):
-        via, to = (0, 1) if kk % 2 == 0 else (1, 0)
+        via, to = (0, 1) if (kk + part) % 2 == 0 else (1, 0)
         arrive(tall(across[via], kk, part), ext_in.at[part, via, kk])
         send_x(branch, kk, part, across[via], across[to], 2)
+
+    def wait_x(kk, part):
+        for slot in range(3):
+            if slot != (kk + part) % 2:
+                arrive(tall(across[slot], kk, part), ext_in.at[part, slot, kk])
+
+    def cross_tall(kk, k, to):
+        total = None
+        for b in range(C):
+            term = mm(rx[b, kk], lig[b, k])
+            total = term if total is None else total + term
+        xs[kk] = total[rank:].astype(BF16)
+        send("mid" if k >= KN else "end", xs.at[kk], xr.at[kk], xr_in.at[kk], (r, to, d), SQ)
+        cx[k] = total[:rank].astype(BF16)
 
     def tests():
         load_ct.wait()
@@ -175,7 +196,7 @@
     def cross_plain(k):
         total = None
         for b in range(C):
-            term = mm(rig[b, k], lig[b, k])
+            term = mm(rig[b, k - KQ], lig[b, k])
             total = term if total is None else total + term
         return total.astype(BF16)
 
@@ -200,8 +221,11 @@
             if k < KN:
                 send_li(B, k, c, (r, edge, d), li_h.at[k])
         load_ri.wait()
-        for k in range(KN):
-            rig[r, k] = ri[k].T
+        for k in range(KQ):
+            qx[k] = ri[k].T
+            send(B, qx.at[k], tall(r, k, 1), ext_in.at[1, 3, k], (r, edge, d), BLK)
+        for k in range(KQ, KN):
+            rig[r, k - KQ] = ri[k].T
             for slot in range(2):
                 send_ri(B, k, r, across[slot], slot)
         for kk in range(KM):
@@ -218,7 +242,8 @@
         for k in range(KN):
             arrive(lig.at[other, k], li_in.at[other, k])
             send_li(B, k, other, (r, edge, d))
-            relay_ri(B, k)
+            if k >= KQ:
+                relay_ri(B, k)
         arrive(tpe, tp_in.at[0])
         both = tpe[...].astype(F32) + tp[...].astype(F32)
         tmid[...] = jnp.where(lower, both[:, 0:half], both[:, half:2 * half])
@@ -227,6 +252,7 @@
         for k in range(1, KN):
             arrive(lig.at[edge, k], li_in.at[edge, k])
             send_li(B, k, edge, (r, other, d))
+        probe_sum(B)
         relay_x(B, 0, 0)
         relay_x(B, 1, 0)
         arrive(tall(r, 0, 1), ext_in.at[1, 3, 0])
@@ -241,7 +267,6 @@
         arrive(tall(r, 1, 1), ext_in.at[1, 3, 1])
         for slot in range(2):
             send_x(B, 1, 1, r, across[slot], slot)
-        probe_sum(B)
         arrive(lig.at[edge, KN], li_in.at[edge, KN])
         send_li(B, KN, edge, (r, other, d))
         for k in range(1, KN):
@@ -254,43 +279,42 @@
         send(B, test.at[1 - h], test.at[1 - h], te_in.at[1 - h], (r, edge, d), sketch * half * 2)
         for kk in range(KM):
             relay_x(B, kk, 1)
-        for k in range(KN):
+        for k in range(KQ, KN):
             wait_ri(k, via_of(k))
-        probe_wait()
         load_li.wait()
         load_mask.wait()
-        for k in range(KN):
+        for k in range(KQ, KN):
             cx[k] = cross_plain(k)
+        probe_wait()
+        for k in range(KQ, KN):
             right_of(k, cx[k])
-        for to in (other, edge):
-            send_crt(B, c, 0, to)
+        for k in range(KQ):
+            arrive(xr.at[k], xr_in.at[k])
+            cx[k] = xr[k]
+            right_of(k, cx[k])
+        send_crt(B, c, 0, other)
+        send_crt(B, c, 0, edge)
         for kk in range(KM):
-            k = KN + kk
             for part in range(2):
-                for slot in range(3):
-                    if slot != via_of(kk):
-                        arrive(tall(across[slot], kk, part), ext_in.at[part, slot, kk])
+                wait_x(kk, part)
             for b in (other, far):
-                arrive(lig.at[b, k], li_in.at[b, k])
-            total = None
-            for b in range(C):
-                term = mm(rx[b, kk], lig[b, k])
-                total = term if total is None else total + term
-            xs[kk] = total[rank:].astype(BF16)
-            send(B, xs.at[kk], xr.at[kk], xr_in.at[kk], (r, edge, d), SQ)
-            cx[k] = total[:rank].astype(BF16)
+                arrive(lig.at[b, KN + kk], li_in.at[b, KN + kk])
+            cross_tall(kk, KN + kk, edge)
         for k in range(KN, K):
             right_of(k, cx[k])
-        for to in (edge, other, far):
-            send_crt(B, c, 1, to)
+        send_crt(B, c, 1, other)
 
     @pl.when(is_end)
     def _():
         B = "end"
         send_li(B, 0, c, (r, near, d), li_h.at[0])
         load_ri.wait()
-        for k in range(KN):
-            rig[r, k] = ri[k].T
+        for k in range(KQ):
+            rx[r, k, 0:rank] = ri[k].T
+            for slot in range(2):
+                send_x(B, k, 0, r, across[slot], slot)
+        for k in range(KQ, KN):
+            rig[r, k - KQ] = ri[k].T
             for slot in range(2):
                 send_ri(B, k, r, across[slot], slot)
         tests()
@@ -298,23 +322,36 @@
         for k in range(1, KN):
             send_li(B, k, c, (r, near, d), li_h.at[k])
         for kk in range(KM):
-            rx[r, kk, 0:rank] = ri[KN + kk].T
-            send(B, tall(r, kk, 0), tall(r, kk, 1), ext_in.at[1, 3, kk], (r, near, d), BLK)
+            ex[kk] = ri[KN + kk].T
+            send(B, ex.at[kk], tall(r, kk, 1), ext_in.at[1, 3, kk], (r, near, d), BLK)
         for k in range(KN, K):
             send_li(B, k, c, (r, near, d), li_h.at[k])
         probes(B)
-        for k in range(KN):
+        for k in range(KQ):
+            relay_x(B, k, 0)
+        for k in range(KQ, KN):
             relay_ri(B, k)
+        for k in range(KQ):
+            arrive(tall(r, k, 1), ext_in.at[1, 3, k])
+            for slot in range(2):
+                send_x(B, k, 1, r, across[slot], slot)
         probe_sum(B)
-        for n in (near, C - 1 - near, other):
-            for k in range(KN):
-                arrive(lig.at[n, k], li_in.at[n, k])
-        for k in range(KN):
-            wait_ri(k, via_of(k))
-        probe_wait()
+        for k in range(KQ):
+            relay_x(B, k, 1)
         load_li.wait()
         load_mask.wait()
-        for k in range(KN):
+        probe_wait()
+        for k in range(KQ):
+            for part in range(2):
+                wait_x(k, part)
+            for n in (near, C - 1 - near, other):
+                arrive(lig.at[n, k], li_in.at[n, k])
+            cross_tall(k, k, near)
+            right_of(k, cx[k])
+        for k in range(KQ, KN):
+            wait_ri(k, via_of(k))
+            for n in (near, C - 1 - near, other):
+                arrive(lig.at[n, k], li_in.at[n, k])
             cx[k] = cross_plain(k)
             right_of(k, cx[k])
         send_crt(B, c, 0, near)
@@ -324,7 +361,7 @@
             arrive(xr.at[kk], xr_in.at[kk])
             cx[KN + kk] = xr[kk]
             right_of(KN + kk, xr[kk])
-        for to in (near, C - 1 - near, other):
+        for to in (other, C - 1 - near, near):
             send_crt(B, c, 1, to)
 
     core_part = None
@@ -345,14 +382,21 @@
         B = "mid"
         arrive(part_of(edge, 0), cr_in.at[edge, 0])
         send_crt(B, edge, 0, other)
-        arrive(part_of(other, 0), cr_in.at[other, 0])
-        send_crt(B, other, 0, edge)
 
     arrive(cpr.at[pl.ds(0, D - 1)], cp_in.at[0])
     core = cpr[0]
     for n in range(1, D):
         core = core + cpr[n]
 
+    def relay_other(part):
+        @pl.when(is_mid)
+        def _():
+            if part == 0:
+                send_crt("mid", c, 1, edge)
+            arrive(part_of(other, part), cr_in.at[other, part])
+            send_crt("mid", other, part, edge)
+
+    relay_other(0)
     gram = mm(core, core, (1, 1), HIGHEST)
     eye = (
         lax.broadcasted_iota(jnp.int32, (rank, rank), 0)
@@ -365,14 +409,16 @@
     start, scales = inverse_schedule(rank)
     rest = eye - start * gram
     inv = (scales[0] * start) * (eye + rest)
-    rest = (1.0 - scales[0]) * eye + scales[0] * mm(rest, rest, precision=HIGHEST)
-    for factor in scales[1:]:
-        both = mm(jnp.concatenate([inv, rest], axis=0), rest, precision=HIGHEST)
+    rest = (1.0 - scales[0]) * eye + scales[0] * mm_split(rest, rest)
+    for step, factor in enumerate(scales[1:]):
+        if step == 5:
+            relay_other(1)
+        both = mm_split(jnp.concatenate([inv, rest], axis=0), rest)
         inv = factor * (inv + both[:rank])
         rest = (1.0 - factor) * eye + factor * both[rank:]
-    for _ in range(1):
-        inv = inv + mm(inv, eye - mm(gram, inv, precision=HIGHEST), precision=HIGHEST)
-    weights = (mm(inv, core, precision=HIGHEST) * (norm[:, 0:1] * rank**0.5)).astype(BF16)
+    solved = mm_split(inv, core)
+    solved = solved + mm_split(inv, core - mm(gram, solved, precision=HIGHEST))
+    weights = (solved * (norm[:, 0:1] * rank**0.5)).astype(BF16)
 
     rows = KN * rank
 
@@ -393,23 +439,34 @@
         arrive(part_of(far, 0), cr_in.at[far, 0])
         send_crt(B, far, 0, edge)
 
-    def relay_z(part):
+    def relay_z(part, branch):
         via, to = (0, 1) if part == 0 else (1, 0)
         arrive(zpart(across[via], part), z_in.at[via, part])
-        send("all", zpart(across[via], part), zpart(across[via], part), z_in.at[2, part],
+        send(branch, zpart(across[via], part), zpart(across[via], part), z_in.at[2, part],
              (across[to], c, d), (KN if part == 0 else KM) * SQ)
 
     part_l = lo_h.shape[1] // D
     place = c * D + d
     owner, slot_l = place // C, lax.rem(place, C)
 
+    def halves(left, right, contract, parts, got, sem, in_s, index):
+        size = left.shape[0] // D
+        if D == 2:
+            for n in (1 - d, d):
+                rows = left[pl.ds(pl.multiple_of(n * size, size), size), :]
+                parts[n, index] = mm(rows, right, contract)
+                if n is not d:
+                    send(sem[0], parts.at[n, index], got.at[index, d], in_s.at[index], (r, c, n), 0, sem[1])
+        else:
+            total = mm(left[...], right, contract)
+            for n in range(D):
+                parts[n, index] = total[n * size:(n + 1) * size]
+            for e in range(1, D):
+                n = lax.rem(d + e, D)
+                send(sem[0], parts.at[n, index], got.at[index, d], in_s.at[index], (r, c, n), 0, sem[1])
+
     def range_mm(j, index):
-        total = mm(lo[...], crt[j], (1, 1))
-        for n in range(D):
-            rps[n, index] = total[n * part_l:(n + 1) * part_l]
-        for e in range(1, D):
-            n = lax.rem(d + e, D)
-            send("rp", rps.at[n, index], rpr.at[index, d], rp_in.at[index], (r, c, n), 0, 4)
+        halves(lo, crt[j], (1, 1), rps, rpr, ("rp", 4), rp_in, index)
 
     def range_out(j, index, first):
         total = rps[d, index]
@@ -425,21 +482,28 @@
             send("all", rsend.at[index], rout.at[slot_l], ro_in.at[slot_l], (r, j, owner), part_l * rank * 2)
 
     range_mm(c, 0)
-    relay_z(0)
-    relay_z(1)
-
-    for o in range(1, C):
-        n = lax.rem(c + o, C)
-        arrive(part_of(n, 1), cr_in.at[n, 1])
+
+    @pl.when(is_mid)
+    def _():
+        relay_z(0, "mid")
+        relay_z(1, "mid")
+        for n in (C - 1 - edge, edge):
+            arrive(part_of(n, 1), cr_in.at[n, 1])
 
     @pl.when(is_end)
     def _():
-        for o in range(1, C):
-            n = lax.rem(c + o, C)
-            arrive(part_of(n, 0), cr_in.at[n, 0])
+        for n in (near, C - 1 - near, other):
+            for part in range(2):
+                arrive(part_of(n, part), cr_in.at[n, part])
 
     for o in range(1, C):
         range_mm(lax.rem(c + o, C), o)
+
+    @pl.when(is_end)
+    def _():
+        relay_z(0, "end")
+        relay_z(1, "end")
+
     for o in range(C):
         range_out(lax.rem(c + o, C), o, o == 0)
 
@@ -448,12 +512,7 @@
     owner_q, slot_q = place_q // R, lax.rem(place_q, R)
 
     def corange_mm(i, index):
-        total = mm(ro[...], zz[i])
-        for n in range(D):
-            qps[n, index] = total[n * part_r:(n + 1) * part_r]
-        for e in range(1, D):
-            n = lax.rem(d + e, D)
-            send("qp", qps.at[n, index], qpr.at[index, d], qp_in.at[index], (r, c, n), 0, 5)
+        halves(ro, zz[i], (1, 0), qps, qpr, ("qp", 5), qp_in, index)
 
     def corange_out(i, index, first):
         total = qps[d, index]
@@ -528,6 +587,7 @@
     assert R == 4 and C == 4 and K % R == 0 and BL == BR and BL % D == 0 and D > 1
     KM = K // 2
     KN = K - KM
+    KQ = KN // 2
     KR = K // R
     dma = pltpu.SemaphoreType.DMA
     vmem = pltpu.VMEM
@@ -540,8 +600,10 @@
         vmem((BR, rank), BF16),
         vmem((BL, sketch), BF16),
         vmem((C, K, BL, rank), BF16),
-        vmem((R, KN, rank, BR), BF16),
+        vmem((R, KN - KQ, rank, BR), BF16),
         vmem((R, KM, 2 * rank, BR), BF16),
+        vmem((KQ, rank, BR), BF16),
+        vmem((KM, rank, BR), BF16),
         vmem((sketch, K * rank), BF16),
         vmem((sketch, K * rank), BF16),
         vmem((sketch, KM * rank), BF16),
@@ -568,7 +630,7 @@
         vmem((R, BR // D, rank), BF16),
         vmem((R, BR // D, rank), BF16),
         dma((7,)), dma((6,)),
-        dma((C, K)), dma((3, KN)), dma((2, 4, KM)), dma((2,)), dma((2,)), dma((1,)), dma((1,)), dma((KM,)),
+        dma((C, K)), dma((3, KN - KQ)), dma((2, 4, KM)), dma((2,)), dma((2,)), dma((1,)), dma((1,)), dma((KM,)),
         dma((1,)), dma((C, 2)), dma((3, 2)), dma((C,)), dma((C,)), dma((R,)), dma((R,)),
     ]
     whole = pl.BlockSpec(memory_space=pltpu.VMEM)

time: 63.5 us -> 58.8 us (0.926)
  Pallas kernels: 61.7 us -> 57 us
    pallas_call x1, Pallas kernels: 61.7 us -> 57 us  [body(): pl.pallas_call(functools.partial(kernel, (R, C, D, K)), out_shape=(out, o...]
where the time goes in v2:
time: 58.8 us; the launch traced here: 58.6 us
  Pallas kernels  57 us (97%)
  other arithmetic  1.04 us (2%)
  between operations  0.64 us (1%)
    pallas_call x1, Pallas kernels, body(): pl.pallas_call(functools.partial(kernel, (R, C, D, K)), out_shape=(out, o...  57 us

profile of v2, /device:TPU:1, one launch (start us, length us, event | category | flops | bytes accessed | tf_op | source)
XLA Modules:
  0.0 58.6 jit_solution(445430280883478915)
XLA Ops:
  0.6 57.0 %shard_map.86 = (bf16[1024,128]{1,0:T(8,128)(2,1)S(1)}, bf16[1024,128]{1,0:T(8,128)(2,1)S(1)}) custom-call(bf16[4,512,128]{2,1,0:T(8,128)(2,1)} %bitcast.12, bf16[4,512,128]{2,1,0:T(8,128)(2,1)} %bitcast.13, bf16[4,512,128]{2,1,0:T(8,128)(2,1)} %bitcast.14, bf16[4,512,128]{2,1,0:T(8,128)(2,1)} %bitcast.15, bf16[512,128]{1,0:T(8,128)(2,1)} %bitcast.17, ...), custom_call_target="tpu_custom_call" | custom-call | tf_op jit(solution)/shard_map/pallas_call | solution.py:638
  57.6 1.0 %bitcast_convert_fusion = (f32[1,1,1024,128]{3,2,1,0:T(8,128)}, f32[1,1,1024,128]{3,2,1,0:T(8,128)}) fusion(bf16[1024,128]{1,0:T(8,128)(2,1)S(1)} %get-tuple-element.5, bf16[1024,128]{1,0:T(8,128)(2,1)S(1)} %get-tuple-element.4), kind=kLoop, calls=%fused_computation | loop fusion | flops 262144 | bytes 1572864 | tf_op jit(solution)/shard_map/convert_element_type | solution.py:652

commit v3 on v2

--- a/solution.py
+++ b/solution.py
@@ -86,6 +86,25 @@
         op.start()
         return op
 
+    bar = pltpu.get_barrier_semaphore()
+
+    def greet(row, col, depth):
+        pl.semaphore_signal(bar, inc=1, device_id=(row, col, depth), device_id_type=MESH)
+
+    def greet_depth(row, col, own):
+        if D <= 4:
+            for e in range(1 if own else 0, D):
+                greet(row, col, lax.rem(d + e, D))
+        else:
+            @pl.loop(1 if own else 0, D)
+            def _(e):
+                greet(row, col, lax.rem(d + e, D))
+
+    greet_depth(r, c, True)
+    for o in range(1, R):
+        greet_depth(lax.rem(r + o, R), c, False)
+    for o in range(1, C):
+        greet_depth(r, lax.rem(c + o, C), False)
     load_ri = load(ri_h, ri, 0)
     load_ct = load(ct_h, ct, 1)
     for k in range(K):
@@ -96,19 +115,7 @@
     load_li = load(li_h, lig.at[c], 5)
     load_mask = load(mask_h, mask, 6)
 
-    bar = pltpu.get_barrier_semaphore()
-
-    @pl.loop(1, R * D)
-    def _(o):
-        n = lax.rem(r * D + d + o, R * D)
-        pl.semaphore_signal(bar, inc=1, device_id=(n // D, c, lax.rem(n, D)), device_id_type=MESH)
-
-    @pl.loop(1, C * D)
-    def _(o):
-        n = lax.rem(c * D + d + o, C * D)
-        pl.semaphore_signal(bar, inc=1, device_id=(r, n // D, lax.rem(n, D)), device_id_type=MESH)
-
-    pl.semaphore_wait(bar, R * D + C * D - 2)
+    pl.semaphore_wait(bar, R * D + C * D - D - 1)
 
     BLK = lig.shape[2] * rank * 2
     SQ = rank * rank * 2
@@ -244,17 +251,17 @@
             send_li(B, k, other, (r, edge, d))
             if k >= KQ:
                 relay_ri(B, k)
+        relay_x(B, 0, 0)
         arrive(tpe, tp_in.at[0])
         both = tpe[...].astype(F32) + tp[...].astype(F32)
         tmid[...] = jnp.where(lower, both[:, 0:half], both[:, half:2 * half])
         tps[...] = jnp.where(lower, both[:, half:2 * half], both[:, 0:half]).astype(BF16)
         send(B, tps, tpo, tp_in.at[1], (r, other, d), sketch * half * 2)
+        relay_x(B, 1, 0)
         for k in range(1, KN):
             arrive(lig.at[edge, k], li_in.at[edge, k])
             send_li(B, k, edge, (r, other, d))
         probe_sum(B)
-        relay_x(B, 0, 0)
-        relay_x(B, 1, 0)
         arrive(tall(r, 0, 1), ext_in.at[1, 3, 0])
         for slot in range(2):
             send_x(B, 0, 1, r, across[slot], slot)
@@ -272,12 +279,13 @@
         for k in range(1, KN):
             arrive(lig.at[far, k], li_in.at[far, k])
             send_li(B, k, far, (r, edge, d))
+        relay_x(B, 0, 1)
         for k in range(KN + 1, K):
             arrive(lig.at[edge, k], li_in.at[edge, k])
             send_li(B, k, edge, (r, other, d))
         arrive(test.at[1 - h], te_in.at[1 - h])
         send(B, test.at[1 - h], test.at[1 - h], te_in.at[1 - h], (r, edge, d), sketch * half * 2)
-        for kk in range(KM):
+        for kk in range(1, KM):
             relay_x(B, kk, 1)
         for k in range(KQ, KN):
             wait_ri(k, via_of(k))
@@ -389,14 +397,14 @@
         core = core + cpr[n]
 
     def relay_other(part):
-        @pl.when(is_mid)
-        def _():
-            if part == 0:
-                send_crt("mid", c, 1, edge)
-            arrive(part_of(other, part), cr_in.at[other, part])
-            send_crt("mid", other, part, edge)
-
-    relay_other(0)
+        arrive(part_of(other, part), cr_in.at[other, part])
+        send_crt("mid", other, part, edge)
+
+
+    @pl.when(is_mid)
+    def _():
+        relay_other(0)
+
     gram = mm(core, core, (1, 1), HIGHEST)
     eye = (
         lax.broadcasted_iota(jnp.int32, (rank, rank), 0)
@@ -412,7 +420,11 @@
     rest = (1.0 - scales[0]) * eye + scales[0] * mm_split(rest, rest)
     for step, factor in enumerate(scales[1:]):
         if step == 5:
-            relay_other(1)
+
+            @pl.when(is_mid)
+            def _():
+                send_crt("mid", c, 1, edge)
+
         both = mm_split(jnp.concatenate([inv, rest], axis=0), rest)
         inv = factor * (inv + both[:rank])
         rest = (1.0 - factor) * eye + factor * both[rank:]
@@ -425,17 +437,22 @@
     def zpart(n, part):
         return zz.at[n, pl.ds(0, rows) if part == 0 else pl.ds(rows, half)]
 
+    def send_z(slot, part):
+        send("all", zpart(r, part), zpart(r, part), z_in.at[slot, part], (across[slot], c, d),
+             (KN if part == 0 else KM) * SQ)
+
     for part in range(2):
         for k in range(KN) if part == 0 else range(KN, K):
             zz[r, pl.ds(k * rank, rank)] = mm(clt[k], weights, (1, 1)).astype(BF16)
-        for slot in range(2):
-            send("all", zpart(r, part), zpart(r, part), z_in.at[slot, part], (across[slot], c, d),
-                 (KN if part == 0 else KM) * SQ)
+        send_z(part, part)
+    for part in range(2):
+        send_z(1 - part, part)
 
     @pl.when(is_mid)
     def _():
         B = "mid"
         far = C - 1 - edge
+        relay_other(1)
         arrive(part_of(far, 0), cr_in.at[far, 0])
         send_crt(B, far, 0, edge)
 
@@ -468,7 +485,7 @@
     def range_mm(j, index):
         halves(lo, crt[j], (1, 1), rps, rpr, ("rp", 4), rp_in, index)
 
-    def range_out(j, index, first):
+    def range_out(j, index, first, branch="all"):
         total = rps[d, index]
         arrive(rpr.at[index, pl.ds(0, D - 1)], rp_in.at[index])
         for e in range(1, D):
@@ -479,33 +496,7 @@
             def _():
                 send("ro", rsend.at[index], rout.at[slot_l], ro_in.at[slot_l], (r, j, owner), part_l * rank * 2, 1)
         else:
-            send("all", rsend.at[index], rout.at[slot_l], ro_in.at[slot_l], (r, j, owner), part_l * rank * 2)
-
-    range_mm(c, 0)
-
-    @pl.when(is_mid)
-    def _():
-        relay_z(0, "mid")
-        relay_z(1, "mid")
-        for n in (C - 1 - edge, edge):
-            arrive(part_of(n, 1), cr_in.at[n, 1])
-
-    @pl.when(is_end)
-    def _():
-        for n in (near, C - 1 - near, other):
-            for part in range(2):
-                arrive(part_of(n, part), cr_in.at[n, part])
-
-    for o in range(1, C):
-        range_mm(lax.rem(c + o, C), o)
-
-    @pl.when(is_end)
-    def _():
-        relay_z(0, "end")
-        relay_z(1, "end")
-
-    for o in range(C):
-        range_out(lax.rem(c + o, C), o, o == 0)
+            send(branch, rsend.at[index], rout.at[slot_l], ro_in.at[slot_l], (r, j, owner), part_l * rank * 2)
 
     part_r = ro_h.shape[1] // D
     place_q = r * D + d
@@ -527,17 +518,65 @@
         else:
             send("all", qsend.at[index], qout.at[slot_q], qo_in.at[slot_q], (i, c, owner_q), part_r * rank * 2)
 
+    order = (c, jnp.where(is_end, near, other), jnp.where(is_end, C - 1 - near, C - 1 - edge),
+             jnp.where(is_end, other, edge))
+
+    range_mm(c, 0)
+
+    @pl.when(is_end)
+    def _():
+        for part in range(2):
+            arrive(part_of(near, part), cr_in.at[near, part])
+
+    range_mm(order[1], 1)
+
+    @pl.when(is_end)
+    def _():
+        for part in range(2):
+            arrive(part_of(C - 1 - near, part), cr_in.at[C - 1 - near, part])
+        range_mm(order[2], 2)
+        relay_z(0, "end")
+        relay_z(1, "end")
+
+    @pl.when(is_mid)
+    def _():
+        relay_z(0, "mid")
+        relay_z(1, "mid")
+
+    for index in range(2):
+        range_out(order[index], index, index == 0)
     corange_mm(r, 0)
+
+    @pl.when(is_end)
+    def _():
+        range_out(order[2], 2, False, "end")
+        for part in range(2):
+            arrive(part_of(other, part), cr_in.at[other, part])
+
+    @pl.when(is_mid)
+    def _():
+        for n in (C - 1 - edge, edge):
+            arrive(part_of(n, 1), cr_in.at[n, 1])
+        range_mm(order[2], 2)
+
+    range_mm(order[3], 3)
     arrive(zpart(across[0], 1), z_in.at[0, 1])
     corange_mm(across[0], 1)
     arrive(zpart(across[1], 0), z_in.at[1, 0])
     corange_mm(across[1], 2)
+
+    @pl.when(is_mid)
+    def _():
+        range_out(order[2], 2, False, "mid")
+
+    range_out(order[3], 3, False)
+    corange_out(r, 0, True)
+    for slot in range(2):
+        corange_out(across[slot], slot + 1, False)
     for part in range(2):
         arrive(zpart(across[2], part), z_in.at[2, part])
     corange_mm(across[2], 3)
-    corange_out(r, 0, True)
-    for slot in range(3):
-        corange_out(across[slot], slot + 1, False)
+    corange_out(across[2], 3, False)
 
     @pl.when(owner == d)
     def _():

time: 58.8 us -> 57.2 us (0.973)
  Pallas kernels: 57 us -> 55.4 us
    pallas_call x1, Pallas kernels: 57 us -> 55.4 us  [body(): pl.pallas_call(functools.partial(kernel, (R, C, D, K)), out_shape=(out, o...]
where the time goes in v3:
time: 57.2 us; the launch traced here: 57.1 us
  Pallas kernels  55.4 us (97%)
  other arithmetic  1.04 us (2%)
  between operations  0.64 us (1%)
    pallas_call x1, Pallas kernels, body(): pl.pallas_call(functools.partial(kernel, (R, C, D, K)), out_shape=(out, o...  55.4 us

profile of v3, /device:TPU:1, one launch (start us, length us, event | category | flops | bytes accessed | tf_op | source)
XLA Modules:
  0.0 57.1 jit_solution(6962161244355923608)
XLA Ops:
  0.6 55.4 %shard_map.86 = (bf16[1024,128]{1,0:T(8,128)(2,1)S(1)}, bf16[1024,128]{1,0:T(8,128)(2,1)S(1)}) custom-call(bf16[4,512,128]{2,1,0:T(8,128)(2,1)} %bitcast.12, bf16[4,512,128]{2,1,0:T(8,128)(2,1)} %bitcast.13, bf16[4,512,128]{2,1,0:T(8,128)(2,1)} %bitcast.14, bf16[4,512,128]{2,1,0:T(8,128)(2,1)} %bitcast.15, bf16[512,128]{1,0:T(8,128)(2,1)} %bitcast.17, ...), custom_call_target="tpu_custom_call" | custom-call | tf_op jit(solution)/shard_map/pallas_call | solution.py:677
  56.0 1.0 %bitcast_convert_fusion = (f32[1,1,1024,128]{3,2,1,0:T(8,128)}, f32[1,1,1024,128]{3,2,1,0:T(8,128)}) fusion(bf16[1024,128]{1,0:T(8,128)(2,1)S(1)} %get-tuple-element.5, bf16[1024,128]{1,0:T(8,128)(2,1)S(1)} %get-tuple-element.4), kind=kLoop, calls=%fused_computation | loop fusion | flops 262144 | bytes 1572864 | tf_op jit(solution)/shard_map/convert_element_type | solution.py:691

commit v4 on v3

--- a/solution.py
+++ b/solution.py
@@ -43,7 +43,7 @@
     out_range, out_corange,
     mask, ruler, lo, ro, ri, rt, ct, lig, rig, rx, qx, ex, tp, tpe, tps, tpo, test, tmid, pps, ppr, probe,
     cx, xs, xr, cps, cpr, crt, clt, zz, rps, rpr, rsend, rout, qps, qpr, qsend, qout,
-    load_s, send_s, li_in, ri_in, ext_in, tp_in, te_in, pp_in, pr_in, xr_in, cp_in, cr_in, z_in,
+    load_s, send_s, li_in, ri_in, ext_in, cp_in, cr_in, z_in,
     rp_in, ro_in, qp_in, qo_in,
 ):
     R, C, D, K = sizes
@@ -168,7 +168,7 @@
             term = mm(rx[b, kk], lig[b, k])
             total = term if total is None else total + term
         xs[kk] = total[rank:].astype(BF16)
-        send("mid" if k >= KN else "end", xs.at[kk], xr.at[kk], xr_in.at[kk], (r, to, d), SQ)
+        send("mid" if k >= KN else "end", xs.at[kk], xr.at[kk], li_in.at[to, kk], (r, to, d), SQ)
         cx[k] = total[:rank].astype(BF16)
 
     def tests():
@@ -183,20 +183,20 @@
         for n in range(R):
             pps[n] = part[:, n * KR * rank:(n + 1) * KR * rank]
         for slot in range(3):
-            send(branch, pps.at[across[slot]], ppr.at[slot], pp_in.at[0],
+            send(branch, pps.at[across[slot]], ppr.at[slot], cr_in.at[c, 0],
                  (across[slot], c, d), KR * SQ * 2)
 
     def probe_sum(branch):
-        arrive(ppr, pp_in.at[0])
+        arrive(ppr, cr_in.at[c, 0])
         total = pps[r]
         for slot in range(3):
             total = total + ppr[slot]
         probe[r] = total.astype(BF16)
         for slot in range(3):
-            send(branch, probe.at[r], probe.at[r], pr_in.at[0], (across[slot], c, d), KR * SQ)
+            send(branch, probe.at[r], probe.at[r], cr_in.at[c, 1], (across[slot], c, d), KR * SQ)
 
     def probe_wait():
-        arrive(probe.at[pl.ds(0, 3)], pr_in.at[0])
+        arrive(probe.at[pl.ds(0, 3)], cr_in.at[c, 1])
 
     scale = (K * D) ** -0.5
 
@@ -252,11 +252,11 @@
             if k >= KQ:
                 relay_ri(B, k)
         relay_x(B, 0, 0)
-        arrive(tpe, tp_in.at[0])
+        arrive(tpe, li_in.at[c, K - 2])
         both = tpe[...].astype(F32) + tp[...].astype(F32)
         tmid[...] = jnp.where(lower, both[:, 0:half], both[:, half:2 * half])
         tps[...] = jnp.where(lower, both[:, half:2 * half], both[:, 0:half]).astype(BF16)
-        send(B, tps, tpo, tp_in.at[1], (r, other, d), sketch * half * 2)
+        send(B, tps, tpo, li_in.at[other, K - 1], (r, other, d), sketch * half * 2)
         relay_x(B, 1, 0)
         for k in range(1, KN):
             arrive(lig.at[edge, k], li_in.at[edge, k])
@@ -267,10 +267,10 @@
             send_x(B, 0, 1, r, across[slot], slot)
         arrive(lig.at[far, 0], li_in.at[far, 0])
         send_li(B, 0, far, (r, edge, d))
-        arrive(tpo, tp_in.at[1])
+        arrive(tpo, li_in.at[c, K - 1])
         test[h] = (tmid[...] + tpo[...].astype(F32)).astype(BF16)
         for to in (edge, other):
-            send(B, test.at[h], test.at[h], te_in.at[h], (r, to, d), sketch * half * 2)
+            send(B, test.at[h], test.at[h], ext_in.at[0, 3, h], (r, to, d), sketch * half * 2)
         arrive(tall(r, 1, 1), ext_in.at[1, 3, 1])
         for slot in range(2):
             send_x(B, 1, 1, r, across[slot], slot)
@@ -283,8 +283,8 @@
         for k in range(KN + 1, K):
             arrive(lig.at[edge, k], li_in.at[edge, k])
             send_li(B, k, edge, (r, other, d))
-        arrive(test.at[1 - h], te_in.at[1 - h])
-        send(B, test.at[1 - h], test.at[1 - h], te_in.at[1 - h], (r, edge, d), sketch * half * 2)
+        arrive(test.at[1 - h], ext_in.at[0, 3, 1 - h])
+        send(B, test.at[1 - h], test.at[1 - h], ext_in.at[0, 3, 1 - h], (r, edge, d), sketch * half * 2)
         for kk in range(1, KM):
             relay_x(B, kk, 1)
         for k in range(KQ, KN):
@@ -297,7 +297,7 @@
         for k in range(KQ, KN):
             right_of(k, cx[k])
         for k in range(KQ):
-            arrive(xr.at[k], xr_in.at[k])
+            arrive(xr.at[k], li_in.at[c, k])
             cx[k] = xr[k]
             right_of(k, cx[k])
         send_crt(B, c, 0, other)
@@ -326,7 +326,7 @@
             for slot in range(2):
                 send_ri(B, k, r, across[slot], slot)
         tests()
-        send(B, tp, tpe, tp_in.at[0], (r, near, d), sketch * K * rank * 2)
+        send(B, tp, tpe, li_in.at[near, K - 2], (r, near, d), sketch * K * rank * 2)
         for k in range(1, KN):
             send_li(B, k, c, (r, near, d), li_h.at[k])
         for kk in range(KM):
@@ -364,9 +364,9 @@
             right_of(k, cx[k])
         send_crt(B, c, 0, near)
         for h in range(2):
-            arrive(test.at[h], te_in.at[h])
+            arrive(test.at[h], ext_in.at[0, 3, h])
         for kk in range(KM):
-            arrive(xr.at[kk], xr_in.at[kk])
+            arrive(xr.at[kk], li_in.at[c, kk])
             cx[KN + kk] = xr[kk]
             right_of(KN + kk, xr[kk])
         for to in (other, C - 1 - near, near):
@@ -466,75 +466,83 @@
     place = c * D + d
     owner, slot_l = place // C, lax.rem(place, C)
 
-    def halves(left, right, contract, parts, got, sem, in_s, index):
+    def halves(left, right, contract, parts, got, sem, in_s, indices):
         size = left.shape[0] // D
+
+        def keep(n, rows):
+            for q, index in enumerate(indices):
+                parts[n, index] = rows[:, q * rank:(q + 1) * rank]
+
+        def share(n):
+            for index in indices:
+                send(sem[0], parts.at[n, index], got.at[index, d], in_s, (r, c, n), 0, sem[1])
+
         if D == 2:
             for n in (1 - d, d):
-                rows = left[pl.ds(pl.multiple_of(n * size, size), size), :]
-                parts[n, index] = mm(rows, right, contract)
+                keep(n, mm(left[pl.ds(pl.multiple_of(n * size, size), size), :], right, contract))
                 if n is not d:
-                    send(sem[0], parts.at[n, index], got.at[index, d], in_s.at[index], (r, c, n), 0, sem[1])
+                    share(n)
         else:
             total = mm(left[...], right, contract)
             for n in range(D):
-                parts[n, index] = total[n * size:(n + 1) * size]
+                keep(n, total[n * size:(n + 1) * size])
             for e in range(1, D):
-                n = lax.rem(d + e, D)
-                send(sem[0], parts.at[n, index], got.at[index, d], in_s.at[index], (r, c, n), 0, sem[1])
-
-    def range_mm(j, index):
-        halves(lo, crt[j], (1, 1), rps, rpr, ("rp", 4), rp_in, index)
+                share(lax.rem(d + e, D))
+
+    def range_mm(js, indices):
+        right = jnp.concatenate([crt[j] for j in js], axis=0)
+        halves(lo, right, (1, 1), rps, rpr, ("rp", 4), rp_in.at[indices[0] // 2], indices)
 
     def range_out(j, index, first, branch="all"):
         total = rps[d, index]
-        arrive(rpr.at[index, pl.ds(0, D - 1)], rp_in.at[index])
+        if index % 2 == 0:
+            arrive(rpr.at[pl.ds(index, 2), pl.ds(0, D - 1)], rp_in.at[index // 2])
         for e in range(1, D):
             total = total + rpr[index, lax.rem(d + e, D)]
         rsend[index] = total.astype(BF16)
         if first:
             @pl.when(owner != d)
             def _():
-                send("ro", rsend.at[index], rout.at[slot_l], ro_in.at[slot_l], (r, j, owner), part_l * rank * 2, 1)
+                send("ro", rsend.at[index], rout.at[slot_l], ro_in.at[0], (r, j, owner), part_l * rank * 2, 1)
         else:
-            send(branch, rsend.at[index], rout.at[slot_l], ro_in.at[slot_l], (r, j, owner), part_l * rank * 2)
+            send(branch, rsend.at[index], rout.at[slot_l], ro_in.at[0], (r, j, owner), part_l * rank * 2)
 
     part_r = ro_h.shape[1] // D
     place_q = r * D + d
     owner_q, slot_q = place_q // R, lax.rem(place_q, R)
 
-    def corange_mm(i, index):
-        halves(ro, zz[i], (1, 0), qps, qpr, ("qp", 5), qp_in, index)
+    def corange_mm(rows, indices):
+        right = jnp.concatenate([zz[i] for i in rows], axis=1)
+        halves(ro, right, (1, 0), qps, qpr, ("qp", 5), qp_in.at[(indices[0] + 1) // 2], indices)
 
     def corange_out(i, index, first):
         total = qps[d, index]
-        arrive(qpr.at[index, pl.ds(0, D - 1)], qp_in.at[index])
+        if index != 2:
+            arrive(qpr.at[pl.ds(index, 2 if index == 1 else 1), pl.ds(0, D - 1)], qp_in.at[(index + 1) // 2])
         for e in range(1, D):
             total = total + qpr[index, lax.rem(d + e, D)]
         qsend[index] = total.astype(BF16)
         if first:
             @pl.when(owner_q != d)
             def _():
-                send("qo", qsend.at[index], qout.at[slot_q], qo_in.at[slot_q], (i, c, owner_q), part_r * rank * 2, 2)
+                send("qo", qsend.at[index], qout.at[slot_q], qo_in.at[0], (i, c, owner_q), part_r * rank * 2, 2)
         else:
-            send("all", qsend.at[index], qout.at[slot_q], qo_in.at[slot_q], (i, c, owner_q), part_r * rank * 2)
+            send("all", qsend.at[index], qout.at[slot_q], qo_in.at[0], (i, c, owner_q), part_r * rank * 2)
 
     order = (c, jnp.where(is_end, near, other), jnp.where(is_end, C - 1 - near, C - 1 - edge),
              jnp.where(is_end, other, edge))
 
-    range_mm(c, 0)
+    corange_mm((r,), (0,))
 
     @pl.when(is_end)
     def _():
         for part in range(2):
             arrive(part_of(near, part), cr_in.at[near, part])
 
-    range_mm(order[1], 1)
+    range_mm(order[:2], (0, 1))
 
     @pl.when(is_end)
     def _():
-        for part in range(2):
-            arrive(part_of(C - 1 - near, part), cr_in.at[C - 1 - near, part])
-        range_mm(order[2], 2)
         relay_z(0, "end")
         relay_z(1, "end")
 
@@ -545,37 +553,30 @@
 
     for index in range(2):
         range_out(order[index], index, index == 0)
-    corange_mm(r, 0)
 
     @pl.when(is_end)
     def _():
-        range_out(order[2], 2, False, "end")
-        for part in range(2):
-            arrive(part_of(other, part), cr_in.at[other, part])
+        for n in (C - 1 - near, other):
+            for part in range(2):
+                arrive(part_of(n, part), cr_in.at[n, part])
 
     @pl.when(is_mid)
     def _():
         for n in (C - 1 - edge, edge):
             arrive(part_of(n, 1), cr_in.at[n, 1])
-        range_mm(order[2], 2)
-
-    range_mm(order[3], 3)
+
+    range_mm(order[2:], (2, 3))
     arrive(zpart(across[0], 1), z_in.at[0, 1])
-    corange_mm(across[0], 1)
     arrive(zpart(across[1], 0), z_in.at[1, 0])
-    corange_mm(across[1], 2)
-
-    @pl.when(is_mid)
-    def _():
-        range_out(order[2], 2, False, "mid")
-
+    corange_mm(across[:2], (1, 2))
+    range_out(order[2], 2, False)
     range_out(order[3], 3, False)
     corange_out(r, 0, True)
     for slot in range(2):
         corange_out(across[slot], slot + 1, False)
     for part in range(2):
         arrive(zpart(across[2], part), z_in.at[2, part])
-    corange_mm(across[2], 3)
+    corange_mm(across[2:], (3,))
     corange_out(across[2], 3, False)
 
     @pl.when(owner == d)
@@ -586,25 +587,23 @@
     def _():
         qout[slot_q] = qsend[0]
 
-    for q in range(C):
-        src = d * C + q
-        mine = jnp.logical_and(src // D == c, lax.rem(src, D) == d)
-
-        @pl.when(jnp.logical_not(mine))
-        def _(q=q):
-            arrive(rout.at[q], ro_in.at[q])
-
-        out_range[q * part_l:(q + 1) * part_l, :] = rout[q]
-    for q in range(R):
-        src = d * R + q
-        mine = jnp.logical_and(src // D == r, lax.rem(src, D) == d)
-
-        @pl.when(jnp.logical_not(mine))
-        def _(q=q):
-            arrive(qout.at[q], qo_in.at[q])
-
-        out_corange[q * part_r:(q + 1) * part_r, :] = qout[q]
-
+    def gather(out, rows, sem, owned):
+        count = rows.shape[0]
+
+        @pl.when(owned)
+        def _():
+            arrive(rows.at[pl.ds(0, count - 1)], sem.at[0])
+
+        @pl.when(jnp.logical_not(owned))
+        def _():
+            arrive(rows, sem.at[0])
+
+        size = rows.shape[1]
+        for q in range(count):
+            out[q * size:(q + 1) * size, :] = rows[q]
+
+    gather(out_range, rout, ro_in, owner == d)
+    gather(out_corange, qout, qo_in, owner_q == d)
     drain(3, cpr.at[pl.ds(0, D - 1)])
     drain(4, rpr.at[:, pl.ds(0, D - 1)])
     drain(5, qpr.at[:, pl.ds(0, D - 1)])
@@ -669,8 +668,8 @@
         vmem((R, BR // D, rank), BF16),
         vmem((R, BR // D, rank), BF16),
         dma((7,)), dma((6,)),
-        dma((C, K)), dma((3, KN - KQ)), dma((2, 4, KM)), dma((2,)), dma((2,)), dma((1,)), dma((1,)), dma((KM,)),
-        dma((1,)), dma((C, 2)), dma((3, 2)), dma((C,)), dma((C,)), dma((R,)), dma((R,)),
+        dma((C, K)), dma((3, KN - KQ)), dma((2, 4, KM)), dma((1,)), dma((C, 2)), dma((3, 2)),
+        dma((2,)), dma((1,)), dma((3,)), dma((1,)),
     ]
     whole = pl.BlockSpec(memory_space=pltpu.VMEM)
     out = jax.ShapeDtypeStruct((BL * C // D, rank), BF16)

time: 57.2 us -> 57.1 us (level)
  no operation moved by 1% of the time
where the time goes in v4:
time: 57.1 us; the launch traced here: 56.9 us
  Pallas kernels  55.3 us (97%)
  other arithmetic  1.04 us (2%)
  between operations  0.64 us (1%)
    pallas_call x1, Pallas kernels, body(): pl.pallas_call(functools.partial(kernel, (R, C, D, K)), out_shape=(out, o...  55.3 us

profile of v4, /device:TPU:1, one launch (start us, length us, event | category | flops | bytes accessed | tf_op | source)
XLA Modules:
  0.0 56.9 jit_solution(16543437243685759604)
XLA Ops:
  0.6 55.3 %shard_map.86 = (bf16[1024,128]{1,0:T(8,128)(2,1)S(1)}, bf16[1024,128]{1,0:T(8,128)(2,1)S(1)}) custom-call(bf16[4,512,128]{2,1,0:T(8,128)(2,1)} %bitcast.12, bf16[4,512,128]{2,1,0:T(8,128)(2,1)} %bitcast.13, bf16[4,512,128]{2,1,0:T(8,128)(2,1)} %bitcast.14, bf16[4,512,128]{2,1,0:T(8,128)(2,1)} %bitcast.15, bf16[512,128]{1,0:T(8,128)(2,1)} %bitcast.17, ...), custom_call_target="tpu_custom_call" | custom-call | tf_op jit(solution)/shard_map/pallas_call | solution.py:676
  55.9 1.0 %bitcast_convert_fusion = (f32[1,1,1024,128]{3,2,1,0:T(8,128)}, f32[1,1,1024,128]{3,2,1,0:T(8,128)}) fusion(bf16[1024,128]{1,0:T(8,128)(2,1)S(1)} %get-tuple-element.5, bf16[1024,128]{1,0:T(8,128)(2,1)S(1)} %get-tuple-element.4), kind=kLoop, calls=%fused_computation | loop fusion | flops 262144 | bytes 1572864 | tf_op jit(solution)/shard_map/convert_element_type | solution.py:690

commit v5 on v4

--- a/solution.py
+++ b/solution.py
@@ -212,6 +212,14 @@
         lanes = pl.ds(k % KR * rank, rank)
         right = (mm(probe[k // KR, :, lanes], cross) * weight).astype(BF16)
         crt[c, :, pl.ds(k * rank, rank)] = right
+
+    def fold(k):
+        weight = mask[0, 0, k].astype(F32) * scale
+        hk, kk = (0, k) if k < KN else (1, k - KN)
+        test_k = test[hk, :, kk * rank:(kk + 1) * rank]
+        clt[k] = (mm(cx[k], test_k, (1, 1)) * weight).astype(BF16)
+        term = mm(crt[c, :, k * rank:(k + 1) * rank], test_k, (1, 1))
+        cps[...] = term if k == 0 else cps[...] + term
 
     def part_of(n, part):
         return crt.at[n, :, pl.ds(0, KN * rank) if part == 0 else pl.ds(KN * rank, half)]
@@ -302,15 +310,19 @@
             right_of(k, cx[k])
         send_crt(B, c, 0, other)
         send_crt(B, c, 0, edge)
+        for k in range(KN):
+            fold(k)
         for kk in range(KM):
             for part in range(2):
                 wait_x(kk, part)
             for b in (other, far):
                 arrive(lig.at[b, KN + kk], li_in.at[b, KN + kk])
             cross_tall(kk, KN + kk, edge)
-        for k in range(KN, K):
-            right_of(k, cx[k])
+            right_of(KN + kk, cx[KN + kk])
+            if kk < KM - 1:
+                fold(KN + kk)
         send_crt(B, c, 1, other)
+        fold(K - 1)
 
     @pl.when(is_end)
     def _():
@@ -365,25 +377,19 @@
         send_crt(B, c, 0, near)
         for h in range(2):
             arrive(test.at[h], ext_in.at[0, 3, h])
+        for k in range(KN):
+            fold(k)
         for kk in range(KM):
             arrive(xr.at[kk], li_in.at[c, kk])
             cx[KN + kk] = xr[kk]
             right_of(KN + kk, xr[kk])
+            fold(KN + kk)
         for to in (other, C - 1 - near, near):
             send_crt(B, c, 1, to)
 
-    core_part = None
-    for k in range(K):
-        weight = mask[0, 0, k].astype(F32) * scale
-        hk, kk = (0, k) if k < KN else (1, k - KN)
-        test_k = test[hk, :, kk * rank:(kk + 1) * rank]
-        clt[k] = (mm(cx[k], test_k, (1, 1)) * weight).astype(BF16)
-        term = mm(crt[c, :, k * rank:(k + 1) * rank], test_k, (1, 1))
-        core_part = term if core_part is None else core_part + term
-    cps[...] = core_part
     for o in range(1, D):
         send("cp", cps, cpr.at[d], cp_in.at[0], (r, c, lax.rem(d + o, D)), 0, 3)
-    cpr[d] = core_part
+    cpr[d] = cps[...]
 
     @pl.when(is_mid)
     def _():

time: 57.1 us -> 56.9 us (level)
  no operation moved by 1% of the time
where the time goes in v5:
time: 56.9 us; the launch traced here: 56.7 us
  Pallas kernels  55.1 us (97%)
  other arithmetic  1.04 us (2%)
  between operations  0.64 us (1%)
    pallas_call x1, Pallas kernels, body(): pl.pallas_call(functools.partial(kernel, (R, C, D, K)), out_shape=(out, o...  55.1 us

profile of v5, /device:TPU:1, one launch (start us, length us, event | category | flops | bytes accessed | tf_op | source)
XLA Modules:
  0.0 56.7 jit_solution(15128804779023284470)
XLA Ops:
  0.6 55.1 %shard_map.86 = (bf16[1024,128]{1,0:T(8,128)(2,1)S(1)}, bf16[1024,128]{1,0:T(8,128)(2,1)S(1)}) custom-call(bf16[4,512,128]{2,1,0:T(8,128)(2,1)} %bitcast.12, bf16[4,512,128]{2,1,0:T(8,128)(2,1)} %bitcast.13, bf16[4,512,128]{2,1,0:T(8,128)(2,1)} %bitcast.14, bf16[4,512,128]{2,1,0:T(8,128)(2,1)} %bitcast.15, bf16[512,128]{1,0:T(8,128)(2,1)} %bitcast.17, ...), custom_call_target="tpu_custom_call" | custom-call | tf_op jit(solution)/shard_map/pallas_call | solution.py:682
  55.7 1.0 %bitcast_convert_fusion = (f32[1,1,1024,128]{3,2,1,0:T(8,128)}, f32[1,1,1024,128]{3,2,1,0:T(8,128)}) fusion(bf16[1024,128]{1,0:T(8,128)(2,1)S(1)} %get-tuple-element.5, bf16[1024,128]{1,0:T(8,128)(2,1)S(1)} %get-tuple-element.4), kind=kLoop, calls=%fused_computation | loop fusion | flops 262144 | bytes 1572864 | tf_op jit(solution)/shard_map/convert_element_type | solution.py:696

commit v6 on v4

--- a/solution.py
+++ b/solution.py
@@ -43,7 +43,7 @@
     out_range, out_corange,
     mask, ruler, lo, ro, ri, rt, ct, lig, rig, rx, qx, ex, tp, tpe, tps, tpo, test, tmid, pps, ppr, probe,
     cx, xs, xr, cps, cpr, crt, clt, zz, rps, rpr, rsend, rout, qps, qpr, qsend, qout,
-    load_s, send_s, li_in, ri_in, ext_in, cp_in, cr_in, z_in,
+    load_s, send_s, li_in, ri_in, ext_in, half_in, cp_in, cr_in, z_in,
     rp_in, ro_in, qp_in, qo_in,
 ):
     R, C, D, K = sizes
@@ -148,19 +148,30 @@
     def tall(ref_row, kk, part):
         return rx.at[ref_row, kk, pl.ds(part * rank, rank)]
 
+    def pieces(branch, owner, kk, part, slot):
+        if branch == "mid" and part == 1 and kk == KM - 1:
+            size = rank // 2
+            return [(rx.at[owner, kk, pl.ds(part * rank + q * size, size)], half_in.at[slot, q]) for q in range(2)]
+        return [(tall(owner, kk, part), ext_in.at[part, slot, kk])]
+
     def send_x(branch, kk, part, owner, to, slot):
-        send(branch, tall(owner, kk, part), tall(owner, kk, part), ext_in.at[part, slot, kk],
-             (to, c, d), BLK)
+        parts = pieces(branch, owner, kk, part, slot)
+        for ref, sem in parts:
+            send(branch, ref, ref, sem, (to, c, d), BLK // len(parts))
 
     def relay_x(branch, kk, part):
         via, to = (0, 1) if (kk + part) % 2 == 0 else (1, 0)
-        arrive(tall(across[via], kk, part), ext_in.at[part, via, kk])
-        send_x(branch, kk, part, across[via], across[to], 2)
-
-    def wait_x(kk, part):
+        got = pieces(branch, across[via], kk, part, via)
+        left = pieces(branch, across[via], kk, part, 2)
+        for (ref, sem), (_, out) in zip(got, left):
+            arrive(ref, sem)
+            send(branch, ref, ref, out, (across[to], c, d), BLK // len(got))
+
+    def wait_x(branch, kk, part):
         for slot in range(3):
             if slot != (kk + part) % 2:
-                arrive(tall(across[slot], kk, part), ext_in.at[part, slot, kk])
+                for ref, sem in pieces(branch, across[slot], kk, part, slot):
+                    arrive(ref, sem)
 
     def cross_tall(kk, k, to):
         total = None
@@ -304,7 +315,7 @@
         send_crt(B, c, 0, edge)
         for kk in range(KM):
             for part in range(2):
-                wait_x(kk, part)
+                wait_x(B, kk, part)
             for b in (other, far):
                 arrive(lig.at[b, KN + kk], li_in.at[b, KN + kk])
             cross_tall(kk, KN + kk, edge)
@@ -351,7 +362,7 @@
         probe_wait()
         for k in range(KQ):
             for part in range(2):
-                wait_x(k, part)
+                wait_x(B, k, part)
             for n in (near, C - 1 - near, other):
                 arrive(lig.at[n, k], li_in.at[n, k])
             cross_tall(k, k, near)
@@ -668,7 +679,7 @@
         vmem((R, BR // D, rank), BF16),
         vmem((R, BR // D, rank), BF16),
         dma((7,)), dma((6,)),
-        dma((C, K)), dma((3, KN - KQ)), dma((2, 4, KM)), dma((1,)), dma((C, 2)), dma((3, 2)),
+        dma((C, K)), dma((3, KN - KQ)), dma((2, 4, KM)), dma((3, 2)), dma((1,)), dma((C, 2)), dma((3, 2)),
         dma((2,)), dma((1,)), dma((3,)), dma((1,)),
     ]
     whole = pl.BlockSpec(memory_space=pltpu.VMEM)

time: 57.1 us -> 57 us (level)
  no operation moved by 1% of the time
where the time goes in v6:
time: 57 us; the launch traced here: 56.8 us
  Pallas kernels  55.1 us (97%)
  other arithmetic  1.04 us (2%)
  between operations  0.64 us (1%)
    pallas_call x1, Pallas kernels, body(): pl.pallas_call(functools.partial(kernel, (R, C, D, K)), out_shape=(out, o...  55.1 us

profile of v6, /device:TPU:1, one launch (start us, length us, event | category | flops | bytes accessed | tf_op | source)
XLA Modules:
  0.0 56.8 jit_solution(4351774123031228424)
XLA Ops:
  0.6 55.1 %shard_map.86 = (bf16[1024,128]{1,0:T(8,128)(2,1)S(1)}, bf16[1024,128]{1,0:T(8,128)(2,1)S(1)}) custom-call(bf16[4,512,128]{2,1,0:T(8,128)(2,1)} %bitcast.12, bf16[4,512,128]{2,1,0:T(8,128)(2,1)} %bitcast.13, bf16[4,512,128]{2,1,0:T(8,128)(2,1)} %bitcast.14, bf16[4,512,128]{2,1,0:T(8,128)(2,1)} %bitcast.15, bf16[512,128]{1,0:T(8,128)(2,1)} %bitcast.17, ...), custom_call_target="tpu_custom_call" | custom-call | tf_op jit(solution)/shard_map/pallas_call | solution.py:687
  55.8 1.0 %bitcast_convert_fusion = (f32[1,1,1024,128]{3,2,1,0:T(8,128)}, f32[1,1,1024,128]{3,2,1,0:T(8,128)}) fusion(bf16[1024,128]{1,0:T(8,128)(2,1)S(1)} %get-tuple-element.5, bf16[1024,128]{1,0:T(8,128)(2,1)S(1)} %get-tuple-element.4), kind=kLoop, calls=%fused_computation | loop fusion | flops 262144 | bytes 1572864 | tf_op jit(solution)/shard_map/convert_element_type | solution.py:701
